TPU v7x, 128 devices: a whole 4x4x4 slice. The times are simulated.
128 devices in a mesh: outer: 4 (over z_lo, core), inner: 32 (over z_hi, y, x).
Axes of the slice: x: 4, y: 4, z: 4 (z_hi: 2, z_lo: 2; z = z_hi * 2 + z_lo), core: 2. Of those that a mesh axis runs over, the one named last changes fastest.
Arguments:
- inputs: bfloat16 [131072, 1024], P(('outer', 'inner')), may hold values from -24 to 24
- queries: bfloat16 [131072, 1024], P(('outer', 'inner')), may hold values from -6 to 6
- keys: bfloat16 [131072, 1024], P(('outer', 'inner')), may hold values from -6 to 6
- values: bfloat16 [131072, 1024], P(('outer', 'inner')), may hold values from -6 to 6
- out_grad: bfloat16 [131072, 1024], P(('outer', 'inner')), may hold values from -6 to 6
- master: float32 [1024, 1024], P('inner'), may hold values from -0.1875 to 0.1875
- moment1: float32 [1024, 1024], P('inner'), may hold values from -6 to 6
- moment2: float32 [1024, 1024], P('inner'), may hold values from 0.05 to 2
Outputs:
- query_grad: bfloat16 [131072, 1024], P(('outer', 'inner'))
- key_grad: bfloat16 [131072, 1024], P(('outer', 'inner'))
- new_master: float32 [1024, 1024], P('inner')
- new_moment1: float32 [1024, 1024], P('inner')
- new_moment2: float32 [1024, 1024], P('inner')
- weights: bfloat16 [1024, 1024], replicated
All inputs are finite; a program needn't handle non-finite values.
Results may differ from a plain program's by a relative error of at most 0.008.
Values may be sent and summed in bfloat16 or wider, within the bound.
A program may use at most 192 MiB of HBM per device.

v0:
```python
import math

import jax
import jax.numpy as jnp
from jax import lax
from jax.sharding import PartitionSpec as P

H = 8
HD = 128
BLK = 512


def entering(array, axis, combine, identity, reverse):
    count, place = (lax.axis_size(axis), lax.axis_index(axis))
    everything = lax.all_gather(array, axis)
    start = jnp.broadcast_to(jnp.asarray(identity, array.dtype), array.shape)

    def turn(k, before):
        at = count - 1 - k if reverse else k
        reached = at > place if reverse else at < place
        new = combine(before, everything[at])
        return jnp.where(reached, new, before)

    return lax.fori_loop(0, count, turn, start)


def add_states(earlier, later):
    return earlier + later


def split_state(state):
    upper = state.astype(jnp.bfloat16)
    lower = (state - upper.astype(jnp.float32)).astype(jnp.bfloat16)
    return (upper, lower)


def state_times_query(form, rows, state):
    upper, lower = split_state(state)
    first = jnp.einsum(form, rows, upper, preferred_element_type=jnp.float32)
    return first + jnp.einsum(form, rows, lower, preferred_element_type=jnp.float32)


def local(inputs, queries, keys, values, out_grad, master, moment1, moment2):
    rows_here = inputs.shape[0]
    width = inputs.shape[1]
    n_outer = lax.axis_size("outer")
    n_inner = lax.axis_size("inner")
    total_tokens = rows_here * n_outer * n_inner
    att_scale = 1.0 / math.sqrt(HD * total_tokens)
    grad_scale = 1.0 / math.sqrt(total_tokens)
    blocks = rows_here // BLK
    shape_four = (blocks, BLK, H, HD)
    query_blocks = queries.reshape(shape_four)
    key_blocks = keys.reshape(shape_four)
    value_blocks = values.reshape(shape_four)
    grad_blocks = out_grad.reshape(shape_four)
    kv_block = jnp.einsum(
        "nthk,nthv->nhkv", key_blocks, value_blocks, preferred_element_type=jnp.float32
    )
    qg_block = jnp.einsum(
        "nthv,nthk->nhvk", grad_blocks, query_blocks, preferred_element_type=jnp.float32
    )
    own_kv = jnp.sum(kv_block, 0)
    own_qg = jnp.sum(qg_block, 0)
    zero_state = jnp.zeros_like(own_kv)
    kv_earlier = entering(own_kv, ("outer", "inner"), add_states, zero_state, False)
    qg_later = entering(own_qg, ("outer", "inner"), add_states, zero_state, True)
    key_value_prior = kv_earlier[None] + jnp.concatenate(
        [zero_state[None], jnp.cumsum(kv_block, 0)[:-1]], 0
    )
    qg_reverse = jnp.cumsum(qg_block[::-1], 0)[::-1]
    qg_after = qg_later[None] + jnp.concatenate([qg_reverse[1:], zero_state[None]], 0)
    causal = jnp.arange(BLK)[:, None] >= jnp.arange(BLK)[None, :]
    query_parts = []
    key_parts = []
    for block_number in range(blocks):
        query_b = query_blocks[block_number]
        key_block_rows = key_blocks[block_number]
        value_block_rows = value_blocks[block_number]
        block_gradient = grad_blocks[block_number]
        scores = jnp.einsum(
            "thv,shv->hts", block_gradient, value_block_rows, preferred_element_type=jnp.float32
        )
        scores = jnp.where(causal[None], scores, 0.0).astype(jnp.bfloat16)
        query_gradient = jnp.einsum(
            "hts,shk->thk", scores, key_block_rows, preferred_element_type=jnp.float32
        )
        query_gradient = query_gradient + state_times_query(
            "rgn,gfn->rgf", block_gradient, key_value_prior[block_number]
        )
        dkey = jnp.einsum("hts,thk->shk", scores, query_b, preferred_element_type=jnp.float32)
        dkey = dkey + state_times_query("shv,hvk->shk", value_block_rows, qg_after[block_number])
        query_parts.append((query_gradient * att_scale).astype(jnp.bfloat16).reshape(BLK, width))
        key_parts.append((dkey * att_scale).astype(jnp.bfloat16).reshape(BLK, width))
    query_grad = jnp.concatenate(query_parts, 0)
    key_grad = jnp.concatenate(key_parts, 0)
    product = lax.dot_general(
        inputs, key_grad, (((0,), (0,)), ((), ())), preferred_element_type=jnp.float32
    )
    shares = lax.psum_scatter(product * grad_scale, "inner", scatter_dimension=0, tiled=True)
    grad = lax.psum(shares, "outer")
    new_moment1 = 0.9 * moment1 + 0.1 * grad
    new_moment2 = 0.95 * moment2 + 0.05 * grad * grad
    new_master = master - 0.01 * (new_moment1 / (jnp.sqrt(new_moment2) + 1e-08) + 0.1 * master)
    weights = lax.all_gather(new_master.astype(jnp.bfloat16), "inner", axis=0, tiled=True)
    return (query_grad, key_grad, new_master, new_moment1, new_moment2, weights)


def solution(mesh):
    in_specs = (
        P(("outer", "inner"), None),
        P(("outer", "inner"), None),
        P(("outer", "inner"), None),
        P(("outer", "inner"), None),
        P(("outer", "inner"), None),
        P("inner", None),
        P("inner", None),
        P("inner", None),
    )
    out_specs = (
        P(("outer", "inner"), None),
        P(("outer", "inner"), None),
        P("inner", None),
        P("inner", None),
        P("inner", None),
        P(),
    )
    return jax.shard_map(local, mesh=mesh, in_specs=in_specs, out_specs=out_specs, check_vma=False)
```

profile of v0, /device:TPU:1, one launch (start us, length us, event | category | flops | bytes accessed | tf_op | source)
XLA Modules:
  0.0 1391.0 jit_solution(7960946358874442010)
XLA Ops:
  7.2 2.4 copy.175
  10.2 2.9 fusion.43
  15.6 3.0 fusion.38
  23.2 3.0 fusion.40
  26.2 2.3 copy.170
  30.8 3.1 fusion.41
  36.1 2.3 copy.171
  38.5 5.1 select_convert_fusion
  43.6 3.4 select_convert_fusion.1
  47.0 353.1 %all-gather.10.cloned.1.call-done = f32[1024,128,128]{2,1,0:T(8,128)} async-done(((f32[8,128,128]{2,1,0:T(8,128)}), f32[1024,128,128]{2,1,0:T(8,128)}) %all-gather.10.cloned.1.call-update) | async-done | bytes 67108880 | tf_op jit(solution)/shard_map/all_gather | solution.py:15
  400.2 160.7 %while.31 = (s32[]{:T(128)}, f32[8,128,128]{2,1,0:T(8,128)S(1)}, s32[]{:T(128)}, f32[128,8,128,128]{3,2,1,0:T(8,128)}, s32[]{:T(128)}, /*index=5*/s32[]{:T(128)}, s32[]{:T(128)}, s32[]{:T(128)}) while((s32[]{:T(128)}, f32[8,128,128]{2,1,0:T(8,128)S(1)}, s32[]{:T(128)}, f32[128,8,128,128]{3,2,1,0:T(8,128)}, s32[]{:T(128)}, ...), condition=%wide.region_6.7_spmd.clone, body=%wide.region_5.6_spmd.clone.sunk | while | flops 393224 | bytes 1573027 | solution.py:24
  569.5 2.4 copy.149
  571.9 5.2 fusion.3
  577.1 2.4 copy.148
  582.2 4.5 multiply_bitcast_fusion
  586.6 5.3 copy.167
  597.4 166.0 %reduce-scatter.4.cloned.1.call-done = f32[32,1024]{1,0:T(8,128)} async-done(((f32[1024,1024]{1,0:T(8,128)}), f32[32,1024]{1,0:T(8,128)}) %reduce-scatter.4.cloned.1.call-update) | async-done | bytes 131088 | tf_op jit(solution)/shard_map/reduce_scatter | solution.py:100
  763.5 3.5 fusion.42
  771.4 48.4 %all-reduce.3.cloned.1.call-done = f32[32,1024]{1,0:T(8,128)} async-done(((f32[32,1024]{1,0:T(8,128)}), f32[32,1024]{1,0:T(8,128)}) %all-reduce.3.cloned.1.call-update) | async-done | bytes 131088 | tf_op jit(solution)/shard_map/psum | solution.py:101
  821.5 384.5 %all-gather.8.cloned.1.call-done = f32[1024,128,128]{2,1,0:T(8,128)} async-done(((f32[8,128,128]{2,1,0:T(8,128)}), f32[1024,128,128]{2,1,0:T(8,128)}) %all-gather.8.cloned.1.call-update) | async-done | bytes 67108880 | tf_op jit(solution)/shard_map/all_gather | solution.py:15
  1206.0 160.2 %while.30 = (s32[]{:T(128)}, f32[8,128,128]{2,1,0:T(8,128)S(1)}, s32[]{:T(128)}, f32[128,8,128,128]{3,2,1,0:T(8,128)}, s32[]{:T(128)}, /*index=5*/s32[]{:T(128)}) while((s32[]{:T(128)}, f32[8,128,128]{2,1,0:T(8,128)S(1)}, s32[]{:T(128)}, f32[128,8,128,128]{3,2,1,0:T(8,128)}, s32[]{:T(128)}, /*index=5*/s32[]{:T(128)}) %tuple.83), condition=%wide.region_2.3_spmd.clone, body=%wide.region_1.0_spmd.clone.sunk | while | flops 393220 | bytes 1572965 | solution.py:24
  1369.6 2.5 fusion.5
  1372.1 2.4 copy.135
  1381.2 3.2 copy.207
  (349 shorter events, 359.4 us)
Async XLA Ops:
  7.2 575.0 %copy-start = (bf16[1024,1024]{1,0:T(8,128)(2,1)S(1)}, bf16[1024,1024]{1,0:T(8,128)(2,1)}, u32[]{:S(2)}) copy-start(bf16[1024,1024]{1,0:T(8,128)(2,1)} %param.12) | copy-start | bytes 6291460
  7.2 393.0 %all-gather.10.cloned.1.call-start = ((), (), s32[]{:S(2)}) async-start(), calls=%async_computation.4 | async-start | bytes 67633152 | tf_op jit(solution)/shard_map/all_gather | solution.py:15
  7.2 2.4 copy-start.11
  13.2 750.2 %reduce-scatter.4.cloned.1.call-start = ((), (), s32[]{:S(2)}) async-start(), calls=%async_computation.5 | async-start | bytes 4325376 | tf_op jit(solution)/shard_map/reduce_scatter | solution.py:100
  38.5 5.1 copy-start.5
  38.5 5.1 copy-start.8
  400.2 160.7 %copy-start.24 = (pred[2]{0:T(512)(128)(4,1)S(1)}, pred[2]{0:T(512)(128)(4,1)}, u32[]{:S(2)}) copy-start(pred[2]{0:T(512)(128)(4,1)} %constant.95.clone.1) | copy-start | bytes 10
  564.2 3.6 copy-start.3
  566.0 1.8 copy-start.15
  569.5 2.4 copy-start.14
  577.1 2.4 copy-start.18
  592.0 227.8 %all-reduce.3.cloned.1.call-start = ((), (), s32[]{:S(2)}) async-start(), calls=%async_computation.1 | async-start | bytes 262144 | tf_op jit(solution)/shard_map/psum | solution.py:101
  593.5 2.0 copy-start.13
  595.5 168.0 %copy-start.20 = (bf16[128,8,8,128]{3,2,1,0:T(8,128)(2,1)S(1)}, bf16[128,8,8,128]{3,2,1,0:T(8,128)(2,1)}, u32[]{:S(2)}) copy-start(bf16[128,8,8,128]{3,2,1,0:T(8,128)(2,1)} %copy.174) | copy-start | bytes 6291460
  763.4 442.5 %all-gather.8.cloned.1.call-start = ((), (), s32[]{:S(2)}) async-start(), calls=%async_computation.3 | async-start | bytes 67633152 | tf_op jit(solution)/shard_map/all_gather | solution.py:15
  767.1 614.1 %all-gather.6.cloned.1.call-start = ((), (), s32[]{:S(2)}) async-start(), calls=%async_computation.2 | async-start | bytes 2162688 | tf_op jit(solution)/shard_map/all_gather | solution.py:105
  769.5 50.3 %copy-start.21 = (f32[32,1024]{1,0:T(8,128)S(1)}, f32[32,1024]{1,0:T(8,128)}, u32[]{:S(2)}) copy-start(f32[32,1024]{1,0:T(8,128)} %param.17) | copy-start | bytes 393220
  769.5 50.3 %copy-start.22 = (f32[32,1024]{1,0:T(8,128)S(1)}, f32[32,1024]{1,0:T(8,128)}, u32[]{:S(2)}) copy-start(f32[32,1024]{1,0:T(8,128)} %param.19) | copy-start | bytes 393220
  769.5 50.3 %copy-start.23 = (f32[32,1024]{1,0:T(8,128)S(1)}, f32[32,1024]{1,0:T(8,128)}, u32[]{:S(2)}) copy-start(f32[32,1024]{1,0:T(8,128)} %param.18) | copy-start | bytes 393220
  1367.4 2.2 copy-start.4
  1372.1 2.4 copy-start.6
  1374.4 2.2 copy-start.2
  1374.8 2.2 copy-start.16
  1381.2 3.2 copy-start.1
  (6 other events, 8.1 us)
Sparse Core Ops, SparseCore 0:
  13.3 386.7 all-gather.9
  592.1 171.2 reduce-scatter.3
  765.9 53.8 all-reduce.2
  821.9 384.0 all-gather.7
  1208.9 70.3 all-gather.5
where the time goes:
time: 1400 us; the launch traced here: 1390 us
  waiting for transfers between devices  952 us (68%)
  other arithmetic  321 us (23%)
  local copies, waits for them, and re-layouts  60.2 us (4%)
  matrix products  36.5 us (3%)
  between operations  14.1 us (1%)
    all_gather x2, waiting for transfers between devices, entering(): everything = lax.all_gather(array, axis)  738 us
    select_n x256, other arithmetic, turn(): return jnp.where(reached, new, before)  314 us
    reduce_scatter x1, waiting for transfers between devices, local(): lax.psum_scatter(product * grad_scale, 'inner', scatter_dimension=0, tile...  166 us
    psum x1, waiting for transfers between devices, local(): grad = lax.psum(shares, 'outer')  48.4 us
    unnamed x60, local copies, waits for them, and re-layouts  33 us
  transfers between devices with their start and end apart: 5, of which 4 were waited for; matrix products, arithmetic and copies ran while one was open for 15% of the time, Pallas kernels for 0%

commit v1 on v0

v1 whole, which is shorter than its diff:
```python
import math

import jax
import jax.numpy as jnp
from jax import lax
from jax.experimental import pallas as pl
from jax.experimental.pallas import tpu as pltpu
from jax.sharding import PartitionSpec as P

H = 8
HD = 128
BLK = 512
HALF = BLK // 2
PLANE = 16
GROUP = 8
MESH = pl.DeviceIdType.MESH
F32 = jnp.float32
BF16 = jnp.bfloat16
ANY = pl.BlockSpec(memory_space=pl.ANY)
VMEM = pl.BlockSpec(memory_space=pltpu.VMEM)


def nt(a, b):
    return lax.dot_general(a, b, (((1,), (1,)), ((), ())), preferred_element_type=F32)


def tn(a, b):
    return lax.dot_general(a, b, (((0,), (0,)), ((), ())), preferred_element_type=F32)


def nn(a, b):
    return lax.dot_general(a, b, (((1,), (0,)), ((), ())), preferred_element_type=F32)


def place():
    outer, inner = lax.axis_index("outer"), lax.axis_index("inner")
    return outer, inner, outer // 2, outer % 2, inner // PLANE, inner % PLANE


def greet(barrier, peers):
    for peer in peers:
        pl.semaphore_signal(barrier, inc=1, device_id=peer, device_id_type=MESH)


def send(src, dst, send_sem, recv_sem, peer):
    copy = pltpu.make_async_remote_copy(
        src_ref=src, dst_ref=dst, send_sem=send_sem, recv_sem=recv_sem, device_id=peer, device_id_type=MESH
    )
    copy.start()
    return copy


def arrived(ref, sem):
    pltpu.make_async_copy(ref, ref, sem).wait()


def scan_kernel(
    q_hbm, k_hbm, v_hbm, g_hbm,
    kvst_ref, qgst_ref, qi_hbm, ki_hbm,
    q, k, v, g, qi, ki, own, got, local, total, totals, back, final, kv0, qg1,
    in_sem, out_sem, s1, r1, s2, r2, s3, r3,
):
    outer, inner, z_lo, core, z_hi, p = place()
    at = z_lo * 4 + core * 2 + z_hi
    plane = [(outer, z_hi * PLANE + (p + o) % PLANE) for o in range(1, PLANE)]
    group = []
    for o in range(1, GROUP):
        other = (at + o) % GROUP
        group.append((other // 2, (other % 2) * PLANE + p))
    barrier = pltpu.get_barrier_semaphore()
    greet(barrier, plane + group)
    loads = []
    for n, (src, dst) in enumerate(((k_hbm, k), (v_hbm, v), (g_hbm, g), (q_hbm, q))):
        copy = pltpu.make_async_copy(src, dst, in_sem.at[n])
        copy.start()
        loads.append(copy)

    loads[0].wait()
    loads[1].wait()

    @pl.loop(0, H)
    def _(h):
        cols = pl.ds(pl.multiple_of(h * HD, HD), HD)
        first = tn(k[0:BLK, cols], v[0:BLK, cols])
        second = tn(k[BLK : 2 * BLK, cols], v[BLK : 2 * BLK, cols])
        kv0[h] = first
        both = (first + second).astype(BF16)
        own[2 * h, 0] = both[0 : HD // 2]
        own[2 * h + 1, 0] = both[HD // 2 :]

    loads[2].wait()
    loads[3].wait()

    @pl.loop(0, H)
    def _(h):
        cols = pl.ds(pl.multiple_of(h * HD, HD), HD)
        first = tn(g[0:BLK, cols], q[0:BLK, cols])
        second = tn(g[BLK : 2 * BLK, cols], q[BLK : 2 * BLK, cols])
        qg1[h] = second
        both = (first + second).astype(BF16)
        own[2 * h, 1] = both[0 : HD // 2]
        own[2 * h + 1, 1] = both[HD // 2 :]

    pl.semaphore_wait(barrier, PLANE - 1 + GROUP - 1)

    sent = []
    for o in range(1, PLANE):
        to = (p + o) % PLANE
        sent.append(send(own.at[to], got.at[p], s1.at[o], r1.at[p], plane[o - 1]))

    rows = lax.broadcasted_iota(jnp.int32, (HALF, HALF), 0)
    lanes = lax.broadcasted_iota(jnp.int32, (HALF, HALF), 1)
    causal = rows >= lanes

    def intra(step):
        top = pl.multiple_of((step // H) * BLK, BLK)
        cols = pl.ds(pl.multiple_of((step % H) * HD, HD), HD)
        a, b = pl.ds(top, HALF), pl.ds(pl.multiple_of(top + HALF, HALF), HALF)
        g0, g1, v0, v1 = g[a, cols], g[b, cols], v[a, cols], v[b, cols]
        s00 = jnp.where(causal, nt(g0, v0), 0.0).astype(BF16)
        s10 = nt(g1, v0).astype(BF16)
        s11 = jnp.where(causal, nt(g1, v1), 0.0).astype(BF16)
        k0, k1, q0, q1 = k[a, cols], k[b, cols], q[a, cols], q[b, cols]
        qi[a, cols] = nn(s00, k0).astype(BF16)
        qi[b, cols] = (nn(s10, k0) + nn(s11, k1)).astype(BF16)
        ki[a, cols] = (tn(s00, q0) + tn(s10, q1)).astype(BF16)
        ki[b, cols] = tn(s11, q1).astype(BF16)

    pl.loop(0, 8)(intra)

    got[p] = own[p]
    for o in range(1, PLANE):
        src = (p + PLANE - o) % PLANE
        arrived(got.at[src], r1.at[src])

    run = jnp.zeros((HD // 2, HD), F32)
    for j in range(PLANE):
        local[j, 0] = run
        run = run + got[j, 0].astype(F32)
    total[0] = run.astype(BF16)
    run = jnp.zeros((HD // 2, HD), F32)
    for j in reversed(range(PLANE)):
        local[j, 1] = run
        run = run + got[j, 1].astype(F32)
    total[1] = run.astype(BF16)

    for o in range(1, GROUP):
        sent.append(send(total, totals.at[at], s2.at[o], r2.at[at], group[o - 1]))

    pl.loop(8, 12)(intra)

    for o in range(1, GROUP):
        src = (at + GROUP - o) % GROUP
        arrived(totals.at[src], r2.at[src])
    totals[at] = total[...]
    before = jnp.zeros((HD // 2, HD), F32)
    after = jnp.zeros((HD // 2, HD), F32)
    for j in range(GROUP):
        before = before + jnp.where(j < at, totals[j, 0].astype(F32), 0.0)
        after = after + jnp.where(j > at, totals[j, 1].astype(F32), 0.0)
    for j in range(PLANE):
        back[j, 0] = (local[j, 0] + before).astype(BF16)
        back[j, 1] = (local[j, 1] + after).astype(BF16)
    for o in range(1, PLANE):
        to = (p + o) % PLANE
        sent.append(send(back.at[to], final.at[p], s3.at[o], r3.at[p], plane[o - 1]))

    pl.loop(12, 16)(intra)
    outs = []
    for n, (src, dst) in enumerate(((qi, qi_hbm), (ki, ki_hbm))):
        copy = pltpu.make_async_copy(src, dst, out_sem.at[n])
        copy.start()
        outs.append(copy)

    final[p] = back[p]
    for o in range(1, PLANE):
        src = (p + PLANE - o) % PLANE
        arrived(final.at[src], r3.at[src])

    for h in range(H):
        for part in range(2):
            piece, half = 2 * h + part, slice(part * HD // 2, (part + 1) * HD // 2)
            kv_in, qg_in = final[piece, 0], final[piece, 1]
            kvst_ref[0, h, half] = kv_in
            kvst_ref[1, h, half] = (kv_in.astype(F32) + kv0[h, half]).astype(BF16)
            qgst_ref[1, h, half] = qg_in
            qgst_ref[0, h, half] = (qg_in.astype(F32) + qg1[h, half]).astype(BF16)

    for copy in sent:
        copy.wait_send()
    for copy in outs:
        copy.wait()


def scan_call(q, k, v, g):
    piece = (2, HD // 2, HD)
    big = pltpu.VMEM(q.shape, BF16)
    state = jax.ShapeDtypeStruct((2, H, HD, HD), BF16)
    full = jax.ShapeDtypeStruct(q.shape, BF16)
    dma = pltpu.SemaphoreType.DMA
    return pl.pallas_call(
        scan_kernel,
        out_shape=(state, state, full, full),
        in_specs=[ANY] * 4,
        out_specs=(VMEM, VMEM, ANY, ANY),
        scratch_shapes=[
            big, big, big, big, big, big,
            pltpu.VMEM((PLANE,) + piece, BF16),
            pltpu.VMEM((PLANE,) + piece, BF16),
            pltpu.VMEM((PLANE,) + piece, F32),
            pltpu.VMEM(piece, BF16),
            pltpu.VMEM((GROUP,) + piece, BF16),
            pltpu.VMEM((PLANE,) + piece, BF16),
            pltpu.VMEM((PLANE,) + piece, BF16),
            pltpu.VMEM((H, HD, HD), F32),
            pltpu.VMEM((H, HD, HD), F32),
            dma((4,)), dma((2,)),
            dma((PLANE,)), dma((PLANE,)), dma((GROUP,)), dma((GROUP,)), dma((PLANE,)), dma((PLANE,)),
        ],
        compiler_params=pltpu.CompilerParams(collective_id=0, has_side_effects=True, vmem_limit_bytes=48 << 20),
        name="scan",
    )(q, k, v, g)


def grads_kernel(scale, kvst, qgst, g, v, qi, ki, dq, dk):
    for h in range(H):
        cols = slice(h * HD, (h + 1) * HD)
        dq[:, cols] = ((qi[:, cols].astype(F32) + nt(g[:, cols], kvst[0, h])) * scale).astype(BF16)
        dk[:, cols] = ((ki[:, cols].astype(F32) + nn(v[:, cols], qgst[0, h])) * scale).astype(BF16)


def grads_call(scale, kvst, qgst, g, v, qi, ki):
    rows, width = g.shape
    tile = 256
    per = BLK // tile
    state = pl.BlockSpec((1, H, HD, HD), lambda i: (i // per, 0, 0, 0))
    band = pl.BlockSpec((tile, width), lambda i: (i, 0))
    full = jax.ShapeDtypeStruct((rows, width), BF16)
    return pl.pallas_call(
        lambda *refs: grads_kernel(scale, *refs),
        out_shape=(full, full),
        grid=(rows // tile,),
        in_specs=[state, state, band, band, band, band],
        out_specs=(band, band),
        compiler_params=pltpu.CompilerParams(vmem_limit_bytes=32 << 20),
        name="grads",
    )(kvst, qgst, g, v, qi, ki)


def update_kernel(
    grad_scale, x_hbm, dk_hbm, master, m1, m2,
    new_master, new_m1, new_m2, w_hbm,
    xs, dk, give, mine, r0, r1, b, r2, c, r3, w, wide, far,
    in_sem, out_sem, s0, q0, s1, q1, s2, q2, s3, q3, s4, q4, s5, q5, s6, q6,
):
    outer, inner, z_lo, core, z_hi, p = place()
    y, x = p // 4, p % 4
    z = z_hi * 2 + z_lo
    partner = (z_lo * 2 + 1 - core, inner)
    along_x = [(outer, z_hi * PLANE + y * 4 + (x + o) % 4) for o in range(1, 4)]
    along_y = [(outer, z_hi * PLANE + ((y + o) % 4) * 4 + x) for o in range(1, 4)]
    seat = core * 4 + z
    group, group_hi = [], []
    for o in range(1, GROUP):
        other = (seat + o) % GROUP
        other_core, other_z = other // 4, other % 4
        group.append(((other_z % 2) * 2 + other_core, (other_z // 2) * PLANE + p))
        group_hi.append(other_z // 2)
    beside = (z + 4 + 2 * z_lo - 1) % 4
    beside_outer, beside_inner = (beside % 2) * 2 + core, (beside // 2) * PLANE
    near_x = [(beside_outer, beside_inner + y * 4 + (x + o) % 4) for o in range(4)]
    near_y = [(beside_outer, beside_inner + ((y + o) % 4) * 4 + x) for o in range(4)]
    peers = along_x + along_y + group + near_x[1:] + near_y[1:]
    barrier = pltpu.get_barrier_semaphore()
    greet(barrier, peers)
    loads = []
    for n, (src, dst) in enumerate(((x_hbm, xs), (dk_hbm, dk))):
        copy = pltpu.make_async_copy(src, dst, in_sem.at[n])
        copy.start()
        loads.append(copy)
    for copy in loads:
        copy.wait()

    def product(half, color, keep):
        cols = pl.ds(pl.multiple_of(half * 512 + color * 256, 256), 256)

        @pl.loop(0, 4)
        def _(m):
            got = tn(xs[:, pl.ds(pl.multiple_of(m * 256, 256), 256)], dk[:, cols]) * grad_scale
            hi = m // 2
            for part in range(8):
                row, at_x = (m % 2) * 2 + part // 4, part % 4
                for lo in range(2):
                    piece = got[part * 32 : part * 32 + 32, lo * 128 : lo * 128 + 128]
                    if color == 0:
                        keep[color, at_x, row, hi, lo] = piece.astype(keep.dtype)
                    else:
                        keep[color, row, at_x, hi, lo] = piece.astype(keep.dtype)

    sent = []
    product(1 - core, 0, give)
    pl.semaphore_wait(barrier, len(peers))
    sent.append(send(give.at[0], r0.at[0], s0.at[0], q0.at[0], partner))
    product(1 - core, 1, give)
    sent.append(send(give.at[1], r0.at[1], s0.at[1], q0.at[1], partner))
    product(core, 0, mine)
    product(core, 1, mine)

    lines = ((x, along_x), (y, along_y))
    for color in range(2):
        here, line = lines[color]
        arrived(r0.at[color], q0.at[color])
        for o in (2, 1, 3):
            to = (here + o) % 4
            b[color, o] = (mine[color, to] + r0[color, to].astype(F32)).astype(BF16)
            sent.append(send(b.at[color, o], r1.at[color, o], s1.at[color, o], q1.at[color, o], line[o - 1]))
        mine[color, here] = mine[color, here] + r0[color, here].astype(F32)
    for color in range(2):
        here = lines[color][0]
        there, line = lines[1 - color]
        for o in range(1, 4):
            arrived(r1.at[color, o], q1.at[color, o])
        mine[color, here] = (
            mine[color, here] + r1[color, 1].astype(F32) + r1[color, 2].astype(F32) + r1[color, 3].astype(F32)
        )
        for o in (2, 1, 3):
            to = (there + o) % 4
            c[color, o] = mine[color, here, to].astype(BF16)
            sent.append(send(c.at[color, o], r2.at[color, o], s2.at[color, o], q2.at[color, o], line[o - 1]))
    for color in range(2):
        here, there = lines[color][0], lines[1 - color][0]
        for o in range(1, 4):
            arrived(r2.at[color, o], q2.at[color, o])
        done = (
            mine[color, here, there] + r2[color, 1].astype(F32) + r2[color, 2].astype(F32) + r2[color, 3].astype(F32)
        ).astype(BF16)
        w[0, color] = done[0]
        w[1, color] = done[1]
    for o in range(1, GROUP):
        sent.append(send(w.at[group_hi[o - 1]], r3.at[seat], s3.at[o], q3.at[seat], group[o - 1]))
    r3[seat] = w[z_hi]
    for o in range(1, GROUP):
        src = (seat + GROUP - o) % GROUP
        arrived(r3.at[src], q3.at[src])

    for t in range(8):
        half, color, lo = t // 4, (t // 2) % 2, t % 2
        cols = slice(t * 128, t * 128 + 128)
        grad = r3[half * 4, color, lo].astype(F32)
        for n in range(1, 4):
            grad = grad + r3[half * 4 + n, color, lo].astype(F32)
        first = 0.9 * m1[:, cols] + 0.1 * grad
        second = 0.95 * m2[:, cols] + 0.05 * grad * grad
        old = master[:, cols]
        new = old - 0.01 * (first / (jnp.sqrt(second) + 1e-08) + 0.1 * old)
        new_m1[:, cols] = first
        new_m2[:, cols] = second
        new_master[:, cols] = new

    for color in range(2):
        here, there = lines[color][0], lines[1 - color][0]
        cols = pl.ds(pl.multiple_of(core * 512 + color * 256, 256), 256)
        wide[color, here, z_hi, there] = new_master[:, cols].astype(BF16)
    for color in range(2):
        here, there = lines[color][0], lines[1 - color][0]
        line = lines[1 - color][1]
        near = near_y if color == 0 else near_x
        spot = wide.at[color, here, z_hi, there]
        for o in (2, 1, 3, 0):
            if o:
                sent.append(send(spot, spot, s4.at[color, 0, o], q4.at[color, 0, o], line[o - 1]))
            sent.append(send(spot, spot, s4.at[color, 1, o], q4.at[color, 1, o], near[o]))
    for color in range(2):
        here, there = lines[color][0], lines[1 - color][0]
        line = lines[color][1]
        for o in range(4):
            src = (there + 4 - o) % 4
            if o:
                arrived(wide.at[color, here, z_hi, src], q4.at[color, 0, o])
            arrived(wide.at[color, here, 1 - z_hi, src], q4.at[color, 1, o])
        spot = wide.at[color, here]
        for o in (2, 1, 3):
            sent.append(send(spot, spot, s5.at[color, o], q5.at[color, o], line[o - 1]))
        sent.append(send(spot, far.at[color, here], s6.at[color, 0], q6.at[color, 0], partner))

    outs = []

    def put(src, half, color, at, n):
        cols = pl.ds(pl.multiple_of(half * 512 + color * 256, 256), 256)
        dst = w_hbm.at[:, :, at, :, cols] if color == 0 else w_hbm.at[:, at, :, :, cols]
        copy = pltpu.make_async_copy(src, dst, out_sem.at[n])
        copy.start()
        outs.append(copy)

    for color in range(2):
        here = lines[color][0]
        put(wide.at[color, here], core, color, here, color * 8)
    for o in (1, 3, 2):
        for color in range(2):
            here = lines[color][0]
            src = (here + 4 - o) % 4
            arrived(wide.at[color, src], q5.at[color, o])
            sent.append(send(wide.at[color, src], far.at[color, src], s6.at[color, o], q6.at[color, o], partner))
            put(wide.at[color, src], core, color, src, color * 8 + o)
    for o in (0, 1, 3, 2):
        for color in range(2):
            here = lines[color][0]
            src = (here + 4 - o) % 4
            arrived(far.at[color, src], q6.at[color, o])
            put(far.at[color, src], 1 - core, color, src, color * 8 + 4 + o)
    for copy in sent:
        copy.wait_send()
    for copy in outs:
        copy.wait()


def update_call(grad_scale, inputs, dk, master, m1, m2):
    rows, width = master.shape
    shard = jax.ShapeDtypeStruct(master.shape, F32)
    dma = pltpu.SemaphoreType.DMA
    tile = (32, 128)
    wide = (2, 4, 2, 4, 32, 256)
    return pl.pallas_call(
        lambda *refs: update_kernel(grad_scale, *refs),
        out_shape=(shard, shard, shard, jax.ShapeDtypeStruct((2, 4, 4, 32, width), BF16)),
        in_specs=[ANY, ANY, VMEM, VMEM, VMEM],
        out_specs=(VMEM, VMEM, VMEM, ANY),
        scratch_shapes=[
            pltpu.VMEM(inputs.shape, BF16),
            pltpu.VMEM(dk.shape, BF16),
            pltpu.VMEM((2, 4, 4, 2, 2) + tile, BF16),
            pltpu.VMEM((2, 4, 4, 2, 2) + tile, F32),
            pltpu.VMEM((2, 4, 4, 2, 2) + tile, BF16),
            pltpu.VMEM((2, 4, 4, 2, 2) + tile, BF16),
            pltpu.VMEM((2, 4, 4, 2, 2) + tile, BF16),
            pltpu.VMEM((2, 4, 2, 2) + tile, BF16),
            pltpu.VMEM((2, 4, 2, 2) + tile, BF16),
            pltpu.VMEM((GROUP, 2, 2) + tile, BF16),
            pltpu.VMEM((2, 2, 2) + tile, BF16),
            pltpu.VMEM(wide, BF16),
            pltpu.VMEM(wide, BF16),
            dma((2,)), dma((16,)),
            dma((2,)), dma((2,)), dma((2, 4)), dma((2, 4)), dma((2, 4)), dma((2, 4)),
            dma((GROUP,)), dma((GROUP,)), dma((2, 2, 4)), dma((2, 2, 4)),
            dma((2, 4)), dma((2, 4)), dma((2, 4)), dma((2, 4)),
        ],
        compiler_params=pltpu.CompilerParams(collective_id=1, has_side_effects=True, vmem_limit_bytes=48 << 20),
        name="update",
    )(inputs, dk, master, m1, m2)


def local(inputs, queries, keys, values, out_grad, master, moment1, moment2):
    total_tokens = inputs.shape[0] * lax.axis_size("outer") * lax.axis_size("inner")
    att_scale = 1.0 / math.sqrt(HD * total_tokens)
    grad_scale = 1.0 / math.sqrt(total_tokens)
    kvst, qgst, qi, ki = scan_call(queries, keys, values, out_grad)
    query_grad, key_grad = grads_call(att_scale, kvst, qgst, out_grad, values, qi, ki)
    new_master, new_m1, new_m2, weights = update_call(grad_scale, inputs, key_grad, master, moment1, moment2)
    return query_grad, key_grad, new_master, new_m1, new_m2, weights.reshape(inputs.shape[1], -1)


def solution(mesh):
    tokens, shard = P(("outer", "inner"), None), P("inner", None)
    return jax.shard_map(
        local,
        mesh=mesh,
        in_specs=(tokens,) * 5 + (shard,) * 3,
        out_specs=(tokens, tokens, shard, shard, shard, P()),
        check_vma=False,
    )
```

time: 1400 us -> 85.8 us (0.06)
  waiting for transfers between devices: 952 us -> 0 us
  other arithmetic: 321 us -> 0 us
  Pallas kernels: 0 us -> 81.6 us
  local copies, waits for them, and re-layouts: 60.2 us -> 3.32 us
  matrix products: 36.5 us -> 0 us
    all_gather x3 -> x0, waiting for transfers between devices: 738 us -> none  [the longest x2 738 us: entering(): everything = lax.all_gather(array, axis)]
    select_n x256 -> x0, other arithmetic: 314 us -> none  [turn(): return jnp.where(reached, new, before)]
    reduce_scatter x1 -> x0, waiting for transfers between devices: 166 us -> none  [local(): lax.psum_scatter(product * grad_scale, 'inner', scatter_dimension=0, tile...]
    pallas_call x0 -> x3, Pallas kernels: none -> 81.6 us  [the longest x1 42 us: update_call(): pl.pallas_call(lambda *refs: update_kernel(grad_scale, *refs), out_shape=...]
    psum x1 -> x0, waiting for transfers between devices: 48.4 us -> none  [local(): grad = lax.psum(shares, 'outer')]
    dot_general x17 -> x0, matrix products: 36.5 us -> none  [the longest x2 8.47 us: local(): jnp.einsum('thv,shv->hts', block_gradient, value_block_rows, preferred_el...]
    unnamed x60 -> x16, local copies, waits for them, and re-layouts: 33 us -> 3.32 us
    slice x9 -> x0, local copies, waits for them, and re-layouts: 17.3 us -> none  [the longest x3 7.58 us: local(): query_b = query_blocks[block_number]]
  transfers between devices with their start and end apart: 5 -> 0, of which waited for: 4 -> 0; matrix products, arithmetic and copies ran while one was open for 15% -> 0% of each run, Pallas kernels for 0% -> 0%
where the time goes in v1:
time: 85.8 us; the launch traced here: 85.6 us
  Pallas kernels  81.6 us (95%)
  local copies, waits for them, and re-layouts  3.32 us (4%)
    pallas_call x1, Pallas kernels, update_call(): pl.pallas_call(lambda *refs: update_kernel(grad_scale, *refs), out_shape=...  42 us
    pallas_call x1, Pallas kernels, scan_call(): pl.pallas_call(scan_kernel, out_shape=(state, state, full, full), in_spec...  36.1 us
    pallas_call x1, Pallas kernels, grads_call(): pl.pallas_call(lambda *refs: grads_kernel(scale, *refs), out_shape=(full,...  3.55 us
    unnamed x16, local copies, waits for them, and re-layouts  3.32 us

profile of v1, /device:TPU:1, one launch (start us, length us, event | category | flops | bytes accessed | tf_op | source)
XLA Modules:
  0.0 85.6 jit_solution(13231590280740831580)
XLA Ops:
  0.6 0.0 copy-start.1
  0.6 0.0 copy-start
  0.7 36.1 %scan.1 = (bf16[2,8,128,128]{3,2,1,0:T(8,128)(2,1)S(1)}, bf16[2,8,128,128]{3,2,1,0:T(8,128)(2,1)S(1)}, bf16[1024,1024]{1,0:T(8,128)(2,1)S(1)}, bf16[1024,1024]{1,0:T(8,128)(2,1)S(1)}) custom-call(bf16[1024,1024]{1,0:T(8,128)(2,1)} %q_hbm.1, bf16[1024,1024]{1,0:T(8,128)(2,1)} %k_hbm.1, bf16[1024,1024]{1,0:T(8,128)(2,1)} %refs_3_.2, bf16[1024,1024]{1,0:T(8,128)(2,1)} %refs_2_.2), custom_call_target="tpu_custom_call" | custom-call | tf_op jit(solution)/shard_map/scan/pallas_call | solution.py:201
  36.7 0.0 copy-done.1
  36.8 0.0 copy-done
  36.8 0.0 copy-start.2
  36.8 0.0 copy-start.3
  36.8 0.0 copy-start.4
  36.8 0.0 copy-start.5
  36.8 3.5 %grads.1 = (bf16[1024,1024]{1,0:T(8,128)(2,1)}, bf16[1024,1024]{1,0:T(8,128)(2,1)}) custom-call(bf16[2,8,128,128]{3,2,1,0:T(8,128)(2,1)S(1)} %get-tuple-element.16.refs_0_, bf16[2,8,128,128]{3,2,1,0:T(8,128)(2,1)S(1)} %get-tuple-element.17.refs_1_, bf16[1024,1024]{1,0:T(8,128)(2,1)S(1)} %copy-done.1, bf16[1024,1024]{1,0:T(8,128)(2,1)S(1)} %copy-done, ...), custom_call_target="tpu_custom_call" | custom-call | tf_op jit(solution)/shard_map/grads/pallas_call | solution.py:239
  40.4 0.0 copy-done.2
  40.4 0.0 copy-done.3
  40.4 0.0 copy-done.4
  40.4 0.0 copy-done.5
  40.4 42.0 %update.1 = (f32[32,1024]{1,0:T(8,128)S(1)}, f32[32,1024]{1,0:T(8,128)S(1)}, f32[32,1024]{1,0:T(8,128)S(1)}, bf16[2,4,4,32,1024]{4,3,2,1,0:T(8,128)(2,1)S(1)}) custom-call(bf16[1024,1024]{1,0:T(8,128)(2,1)S(1)} %copy-done.2, bf16[1024,1024]{1,0:T(8,128)(2,1)} %get-tuple-element.33.refs_1_, f32[32,1024]{1,0:T(8,128)S(1)} %copy-done.3, ...), custom_call_target="tpu_custom_call" | custom-call | tf_op jit(solution)/shard_map/update/pallas_call | solution.py:423
  82.4 0.7 copy.18
  83.0 0.7 copy.19
  83.7 0.7 copy.20
  84.3 1.3 %copy.21 = bf16[1024,1024]{1,0:T(8,128)(2,1)} copy(bf16[1024,1024]{1,0:T(8,128)(2,1)S(1)} %bitcast.1) | data formatting | bytes 4194304
Async XLA Ops:
  0.6 36.1 %copy-start.1 = (bf16[1024,1024]{1,0:T(8,128)(2,1)S(1)}, bf16[1024,1024]{1,0:T(8,128)(2,1)}, u32[]{:S(2)}) copy-start(bf16[1024,1024]{1,0:T(8,128)(2,1)} %refs_2_.2) | copy-start | bytes 6291460
  0.6 36.1 %copy-start = (bf16[1024,1024]{1,0:T(8,128)(2,1)S(1)}, bf16[1024,1024]{1,0:T(8,128)(2,1)}, u32[]{:S(2)}) copy-start(bf16[1024,1024]{1,0:T(8,128)(2,1)} %refs_3_.2) | copy-start | bytes 6291460
  36.8 3.6 %copy-start.2 = (bf16[1024,1024]{1,0:T(8,128)(2,1)S(1)}, bf16[1024,1024]{1,0:T(8,128)(2,1)}, u32[]{:S(2)}) copy-start(bf16[1024,1024]{1,0:T(8,128)(2,1)} %refs_0_.1) | copy-start | bytes 6291460
  36.8 3.6 %copy-start.3 = (f32[32,1024]{1,0:T(8,128)S(1)}, f32[32,1024]{1,0:T(8,128)}, u32[]{:S(2)}) copy-start(f32[32,1024]{1,0:T(8,128)} %refs_2_.3) | copy-start | bytes 393220
  36.8 3.6 %copy-start.4 = (f32[32,1024]{1,0:T(8,128)S(1)}, f32[32,1024]{1,0:T(8,128)}, u32[]{:S(2)}) copy-start(f32[32,1024]{1,0:T(8,128)} %refs_3_.3) | copy-start | bytes 393220
  36.8 3.6 %copy-start.5 = (f32[32,1024]{1,0:T(8,128)S(1)}, f32[32,1024]{1,0:T(8,128)}, u32[]{:S(2)}) copy-start(f32[32,1024]{1,0:T(8,128)} %refs_4_.1) | copy-start | bytes 393220

commit v2 on v0

v2 whole, which is shorter than its diff:
```python
import math

import jax
import jax.numpy as jnp
from jax import lax
from jax.experimental import pallas as pl
from jax.experimental.pallas import tpu as pltpu
from jax.sharding import PartitionSpec as P

H = 8
HD = 128
BLK = 512
HALF = BLK // 2
PLANE = 16
N1, N2, K1, M1, M2 = 6, 10, 4, 4, 10
GROUP = 8
MESH = pl.DeviceIdType.MESH
F32 = jnp.float32
BF16 = jnp.bfloat16
ANY = pl.BlockSpec(memory_space=pl.ANY)
VMEM = pl.BlockSpec(memory_space=pltpu.VMEM)


def nt(a, b):
    return lax.dot_general(a, b, (((1,), (1,)), ((), ())), preferred_element_type=F32)


def tn(a, b):
    return lax.dot_general(a, b, (((0,), (0,)), ((), ())), preferred_element_type=F32)


def nn(a, b):
    return lax.dot_general(a, b, (((1,), (0,)), ((), ())), preferred_element_type=F32)


def place():
    outer, inner = lax.axis_index("outer"), lax.axis_index("inner")
    return outer, inner, outer // 2, outer % 2, inner // PLANE, inner % PLANE


def greet(barrier, peers):
    for peer in peers:
        pl.semaphore_signal(barrier, inc=1, device_id=peer, device_id_type=MESH)


def send(src, dst, send_sem, recv_sem, peer):
    copy = pltpu.make_async_remote_copy(
        src_ref=src, dst_ref=dst, send_sem=send_sem, recv_sem=recv_sem, device_id=peer, device_id_type=MESH
    )
    copy.start()
    return copy


def arrived(ref, sem):
    pltpu.make_async_copy(ref, ref, sem).wait()


def adam(grad, master, m1, m2):
    first = 0.9 * m1 + 0.1 * grad
    second = 0.95 * m2 + 0.05 * grad * grad
    new = master - 0.01 * (first / (jnp.sqrt(second) + 1e-08) + 0.1 * master)
    return new, first, second


def diagonal(first, second):
    zero = jnp.zeros_like(first)
    return jnp.concatenate([jnp.concatenate([first, zero], 1), jnp.concatenate([zero, second], 1)], 0)


def kernel(
    att_scale, grad_scale,
    x_hbm, q_hbm, k_hbm, v_hbm, g_hbm, master, m1, m2,
    dq_hbm, dk_hbm, w_hbm, grad_ref,
    x, q, k, v, g, xt, ki, xv, dq, dk, pre, scores, qg1, kv0,
    own, got, local, total, totals, back, final,
    give, mine, r0, r1, b, r2, c, r3, w, done, summed, other_sum, wide, far,
    in_sem, out_sem, a1, e1, a2, e2, a3, e3,
    s0, q0, s1, q1, s2, q2, s3, q3, s4, q4, s5, q5, s6, q6, pair_sem,
):
    outer, inner, z_lo, core, z_hi, p = place()
    at_y, at_x = p // 4, p % 4
    z = z_hi * 2 + z_lo
    at = z_lo * 4 + core * 2 + z_hi
    plane = [(outer, z_hi * PLANE + (p + o) % PLANE) for o in range(1, PLANE)]
    ranked = []
    for o in range(1, GROUP):
        other = (at + o) % GROUP
        ranked.append((other // 2, (other % 2) * PLANE + p))
    partner = (z_lo * 2 + 1 - core, inner)
    along_x = [(outer, z_hi * PLANE + at_y * 4 + (at_x + o) % 4) for o in range(1, 4)]
    along_y = [(outer, z_hi * PLANE + ((at_y + o) % 4) * 4 + at_x) for o in range(1, 4)]
    beside = (z + 4 + 2 * z_lo - 1) % 4
    beside_outer, beside_inner = (beside % 2) * 2 + core, (beside // 2) * PLANE
    near_x = [(beside_outer, beside_inner + at_y * 4 + (at_x + o) % 4) for o in range(4)]
    near_y = [(beside_outer, beside_inner + ((at_y + o) % 4) * 4 + at_x) for o in range(4)]
    peers = plane + ranked + near_x[1:] + near_y[1:]
    barrier = pltpu.get_barrier_semaphore()
    greet(barrier, peers)
    loads = []
    for n, (src, dst) in enumerate(((g_hbm, g), (q_hbm, q), (k_hbm, k), (v_hbm, v), (x_hbm, x))):
        copy = pltpu.make_async_copy(src, dst, in_sem.at[n])
        copy.start()
        loads.append(copy)
    sent = []
    QG, KV = 0, 1

    def head_cols(h):
        return pl.ds(pl.multiple_of(h * HD, HD), HD)

    def states(stream, left, right, keep, kept):
        @pl.loop(0, H)
        def _(h):
            cols = head_cols(h)
            blocks = [tn(left[n * BLK : (n + 1) * BLK, cols], right[n * BLK : (n + 1) * BLK, cols]) for n in range(2)]
            keep[h] = blocks[kept].astype(keep.dtype)
            both = (blocks[0] + blocks[1]).astype(BF16)
            own[stream, 2 * h] = both[0 : HD // 2]
            own[stream, 2 * h + 1] = both[HD // 2 :]

    def spread(stream):
        for o in range(1, PLANE):
            to = (p + o) % PLANE
            sent.append(send(own.at[stream, to], got.at[stream, p], a1.at[stream, o], e1.at[stream, p], plane[o - 1]))
        got[stream, p] = own[stream, p]

    def gather(stream):
        for o in range(1, PLANE):
            src = (p + PLANE - o) % PLANE
            arrived(got.at[stream, src], e1.at[stream, src])
        run = jnp.zeros((HD // 2, HD), F32)
        for j in range(PLANE) if stream == KV else reversed(range(PLANE)):
            local[stream, j] = run
            run = run + got[stream, j].astype(F32)
        total[stream] = run.astype(BF16)

    def wanted(stream, here, there):
        return there < here if stream == KV else there > here

    def share(stream):
        for o in range(1, GROUP):
            other = (at + o) % GROUP

            @pl.when(wanted(stream, other, at))
            def _():
                send(total.at[stream], totals.at[stream, at], a2.at[stream, o], e2.at[stream, at], ranked[o - 1])

    def shared(stream):
        for o in range(1, GROUP):
            other = (at + o) % GROUP

            @pl.when(wanted(stream, other, at))
            def _():
                arrived(total.at[stream], a2.at[stream, o])

    def answer(stream):
        for j in range(GROUP):
            @pl.when(wanted(stream, at, j))
            def _():
                arrived(totals.at[stream, j], e2.at[stream, j])

            @pl.when(jnp.logical_not(wanted(stream, at, j)))
            def _():
                totals[stream, j] = jnp.zeros((HD // 2, HD), BF16)
        base = totals[stream, 0].astype(F32)
        for j in range(1, GROUP):
            base = base + totals[stream, j].astype(F32)
        for j in range(PLANE):
            back[stream, j] = (local[stream, j] + base).astype(BF16)
        for o in range(1, PLANE):
            to = (p + o) % PLANE
            sent.append(send(back.at[stream, to], final.at[stream, p], a3.at[stream, o], e3.at[stream, p], plane[o - 1]))
        final[stream, p] = back[stream, p]

    def answered(stream):
        for o in range(1, PLANE):
            src = (p + PLANE - o) % PLANE
            arrived(final.at[stream, src], e3.at[stream, src])

    rows = lax.broadcasted_iota(jnp.int32, (HALF, HALF), 0)
    lanes = lax.broadcasted_iota(jnp.int32, (HALF, HALF), 1)
    causal = rows >= lanes

    def bands(step):
        top = pl.multiple_of((step // H) * BLK, BLK)
        return pl.ds(top, HALF), pl.ds(pl.multiple_of(top + HALF, HALF), HALF), head_cols(step % H)

    def key_side(step):
        top, low, cols = bands(step)
        g0, g1, v0, v1 = g[top, cols], g[low, cols], v[top, cols], v[low, cols]
        s00 = jnp.where(causal, nt(g0, v0), 0.0).astype(BF16)
        s10 = nt(g1, v0).astype(BF16)
        s11 = jnp.where(causal, nt(g1, v1), 0.0).astype(BF16)
        scores[step, 0], scores[step, 1], scores[step, 2] = s00, s10, s11
        q0, q1 = q[top, cols], q[low, cols]
        ki[top, cols] = (tn(s00, q0) + tn(s10, q1)).astype(BF16)
        ki[low, cols] = tn(s11, q1).astype(BF16)

    def state_of(stream, h):
        return final[stream, pl.ds(2 * h, 2)].reshape(HD, HD)

    def key_end(step):
        top, low, cols = bands(step)
        h = step % H
        state = (state_of(QG, h).astype(F32) + jnp.where(step < H, qg1[h].astype(F32), 0.0)).astype(BF16)
        for band in (top, low):
            dk[band, cols] = ((ki[band, cols].astype(F32) + nn(v[band, cols], state)) * att_scale).astype(BF16)

    def query_end(step):
        top, low, cols = bands(step)
        h = step % H
        state = (state_of(KV, h).astype(F32) + jnp.where(step >= H, kv0[h], 0.0)).astype(BF16)
        k0, k1 = k[top, cols], k[low, cols]
        dq[top, cols] = ((nn(scores[step, 0], k0) + nt(g[top, cols], state)) * att_scale).astype(BF16)
        dq[low, cols] = (
            (nn(scores[step, 1], k0) + nn(scores[step, 2], k1) + nt(g[low, cols], state)) * att_scale
        ).astype(BF16)

    def band_and_pair(step, half):
        pair = half * 2 + step % 2
        return pl.ds(pl.multiple_of((step // 2) * 256, 256), 256), pl.ds(pl.multiple_of(pair * 256, 256), 256), pair

    def before_scan(half, whole):
        def body(step):
            band, cols, pair = band_and_pair(step, half)
            upper = nn(xt[band, 0:BLK], v[0:BLK, cols])
            lower = nn(xt[band, BLK : 2 * BLK], v[BLK : 2 * BLK, cols])
            xv[band, cols] = (upper + lower).astype(BF16)
            known = nn(upper.astype(BF16), diagonal(qg1[2 * pair], qg1[2 * pair + 1]))
            if whole:
                known = known + nn(xt[band, :], ki[:, cols])
            pre[band, cols] = known

        return body

    def rest_of(half):
        def body(step):
            band, cols, pair = band_and_pair(step, half)
            pre[band, cols] = pre[band, cols] + nn(xt[band, :], ki[:, cols])

        return body

    def after_scan(half, color, keep):
        pair = half * 2 + color
        cols = pl.ds(pl.multiple_of(pair * 256, 256), 256)
        state = diagonal(state_of(QG, 2 * pair), state_of(QG, 2 * pair + 1))

        @pl.loop(0, 4, unroll=2)
        def _(m):
            band = pl.ds(pl.multiple_of(m * 256, 256), 256)
            made = (pre[band, cols] + nn(xv[band, cols], state)) * (att_scale * grad_scale)
            hi = m // 2
            for part in range(8):
                in_y, in_x = (m % 2) * 2 + part // 4, part % 4
                for lo in range(2):
                    piece = made[part * 32 : part * 32 + 32, lo * 128 : lo * 128 + 128].astype(keep.dtype)
                    if color == 0:
                        keep[color, in_x, in_y, hi, lo] = piece
                    else:
                        keep[color, in_y, in_x, hi, lo] = piece

    loads[0].wait()
    loads[1].wait()
    states(QG, g, q, qg1, 1)
    pl.semaphore_wait(barrier, len(peers))
    spread(QG)
    loads[2].wait()
    loads[3].wait()
    states(KV, k, v, kv0, 0)
    spread(KV)
    loads[4].wait()
    pl.loop(0, N1, unroll=2)(key_side)
    gather(QG)
    share(QG)
    pl.loop(N1, N2, unroll=2)(key_side)
    gather(KV)
    share(KV)
    answer(QG)

    @pl.loop(0, 4)
    def _(m):
        band = pl.ds(pl.multiple_of(m * 256, 256), 256)
        xt[band, :] = x[:, band].T

    pl.loop(N2, 16, unroll=2)(key_side)
    answer(KV)
    pl.loop(0, 8, unroll=2)(before_scan(1 - core, True))
    pl.loop(0, 8, unroll=2)(before_scan(core, False))
    answered(QG)

    for color in range(2):
        after_scan(1 - core, color, give)
        sent.append(send(give.at[color], r0.at[color], s0.at[color], q0.at[color], partner))
    pl.loop(0, 8, unroll=2)(rest_of(core))
    for color in range(2):
        after_scan(core, color, mine)

    lines = ((at_x, along_x), (at_y, along_y))
    def ahead(color, n, to, rows, peer, relay=None):
        part = mine[color, to, rows] + r0[color, to, rows].astype(F32)
        if relay is not None:
            arrived(r1.at[color, relay], q1.at[color, relay])
            part = part + r1[color, relay].astype(F32)
        b[color, n] = part.astype(BF16)
        sent.append(send(b.at[color, n], r1.at[color, n], s1.at[color, n], q1.at[color, n], peer))

    first, second = slice(0, 2), slice(2, 4)
    for color in range(2):
        here, line = lines[color]
        arrived(r0.at[color], q0.at[color])
        up, across, down = (here + 1) % 4, (here + 2) % 4, (here + 3) % 4
        ahead(color, 0, across, first, line[0])
        ahead(color, 1, across, second, line[2])
        ahead(color, 2, up, second, line[0])
        ahead(color, 4, down, first, line[2])
        mine[color, here] = mine[color, here] + r0[color, here].astype(F32)
    pl.loop(0, K1, unroll=2)(key_end)
    for color in range(2):
        here, line = lines[color]
        ahead(color, 3, (here + 1) % 4, first, line[0], 0)
        ahead(color, 5, (here + 3) % 4, second, line[2], 1)
    pl.loop(K1, 16, unroll=2)(key_end)
    outs = []
    copy = pltpu.make_async_copy(dk, dk_hbm, out_sem.at[16])
    copy.start()
    outs.append(copy)
    answered(KV)
    pl.loop(0, M1, unroll=2)(query_end)
    for color in range(2):
        here = lines[color][0]
        there, line = lines[1 - color]
        for n in range(2, 6):
            arrived(r1.at[color, n], q1.at[color, n])
        mine[color, here, first] = mine[color, here, first] + r1[color, 3].astype(F32) + r1[color, 4].astype(F32)
        mine[color, here, second] = mine[color, here, second] + r1[color, 2].astype(F32) + r1[color, 5].astype(F32)
        for o in (2, 1, 3):
            to = (there + o) % 4
            c[color, o] = mine[color, here, to].astype(BF16)
            sent.append(send(c.at[color, o], r2.at[color, o], s2.at[color, o], q2.at[color, o], line[o - 1]))
    for color in range(2):
        here, there = lines[color][0], lines[1 - color][0]
        for o in range(1, 4):
            arrived(r2.at[color, o], q2.at[color, o])
        done[:, color] = (
            mine[color, here, there] + r2[color, 1].astype(F32) + r2[color, 2].astype(F32) + r2[color, 3].astype(F32)
        )
    w[...] = done[...].astype(BF16)
    for o in (2, 1, 3):
        to = (z + o) % 4
        peer = ((to % 2) * 2 + core, (to // 2) * PLANE + p)
        sent.append(send(w.at[to // 2], r3.at[o], s3.at[o], q3.at[o], peer))
    for o in range(1, 4):
        arrived(r3.at[o], q3.at[o])
    summed[...] = done[z_hi] + r3[1].astype(F32) + r3[2].astype(F32) + r3[3].astype(F32)
    fresh = []
    for t in range(4):
        cols = pl.ds(pl.multiple_of(core * 512 + t * 128, 128), 128)
        grad = summed[t // 2, t % 2]
        grad_ref[:, cols] = grad
        fresh.append(adam(grad, master[:, cols], m1[:, cols], m2[:, cols])[0].astype(BF16))

    for color in range(2):
        here, there = lines[color][0], lines[1 - color][0]
        for lo in range(2):
            t = color * 2 + lo
            wide[color, here, z_hi, there, :, lo * 128 : lo * 128 + 128] = fresh[t]
    for color in range(2):
        here, there = lines[color][0], lines[1 - color][0]
        line = lines[1 - color][1]
        near = near_y if color == 0 else near_x
        spot = wide.at[color, here, z_hi, there]
        for o in (2, 1, 3, 0):
            if o:
                sent.append(send(spot, spot, s4.at[color, 0, o], q4.at[color, 0, o], line[o - 1]))
            sent.append(send(spot, spot, s4.at[color, 1, o], q4.at[color, 1, o], near[o]))
    sent.append(send(summed, other_sum, pair_sem.at[0], pair_sem.at[1], partner))
    def onward(color, n, src, hi, peer):
        spot = wide.at[color, src, hi]
        sent.append(send(spot, spot, s5.at[color, n], q5.at[color, n], peer))

    for near in range(2):
        hi = (z_hi + near) % 2
        for color in range(2):
            here, there = lines[color][0], lines[1 - color][0]
            line = lines[color][1]
            for o in range(near == 0, 4):
                arrived(wide.at[color, here, hi, (there + 4 - o) % 4], q4.at[color, near, o])
            onward(color, 2 * near, here, hi, line[2 * near])
            onward(color, 2 * near + 1, here, hi, line[2 - 2 * near])
    for color in range(2):
        here = lines[color][0]
        sent.append(send(wide.at[color, here], far.at[color, here], s6.at[color, 0], q6.at[color, 0], partner))

    def put(src, half, color, at, n):
        cols = pl.ds(pl.multiple_of(half * 512 + color * 256, 256), 256)
        dst = w_hbm.at[:, :, at, :, cols] if color == 0 else w_hbm.at[:, at, :, :, cols]
        copy = pltpu.make_async_copy(src, dst, out_sem.at[n])
        copy.start()
        outs.append(copy)

    pl.loop(M1, M2, unroll=2)(query_end)
    for color in range(2):
        here, line = lines[color]
        put(wide.at[color, here], core, color, here, color * 8)
        arrived(wide.at[color, (here + 3) % 4, z_hi], q5.at[color, 0])
        onward(color, 4, (here + 3) % 4, z_hi, line[0])
    for color in range(2):
        here, line = lines[color]
        arrived(wide.at[color, (here + 1) % 4, 1 - z_hi], q5.at[color, 2])
        onward(color, 5, (here + 1) % 4, 1 - z_hi, line[2])
    pl.loop(M2, 16, unroll=2)(query_end)
    copy = pltpu.make_async_copy(dq, dq_hbm, out_sem.at[17])
    copy.start()
    outs.append(copy)
    for o in (1, 3, 2):
        for color in range(2):
            here = lines[color][0]
            src = (here + 4 - o) % 4
            if o == 1:
                arrived(wide.at[color, src, 1 - z_hi], q5.at[color, 3])
            if o == 3:
                arrived(wide.at[color, src, z_hi], q5.at[color, 1])
            if o == 2:
                arrived(wide.at[color, src, z_hi], q5.at[color, 4])
                arrived(wide.at[color, src, 1 - z_hi], q5.at[color, 5])
            sent.append(send(wide.at[color, src], far.at[color, src], s6.at[color, o], q6.at[color, o], partner))
            put(wide.at[color, src], core, color, src, color * 8 + o)
    for o in (0, 1, 3, 2):
        for color in range(2):
            here = lines[color][0]
            src = (here + 4 - o) % 4
            arrived(far.at[color, src], q6.at[color, o])
            put(far.at[color, src], 1 - core, color, src, color * 8 + 4 + o)
    arrived(other_sum, pair_sem.at[1])
    for t in range(4):
        cols = pl.ds(pl.multiple_of((1 - core) * 512 + t * 128, 128), 128)
        grad_ref[:, cols] = other_sum[t // 2, t % 2]
    for copy in sent:
        copy.wait_send()
    shared(QG)
    shared(KV)
    for copy in outs:
        copy.wait()


def kernel_call(att_scale, grad_scale, inputs, q, k, v, g, master, m1, m2):
    width = inputs.shape[1]
    dma = pltpu.SemaphoreType.DMA
    tile = (32, 128)
    piece = (HD // 2, HD)
    wide = (2, 4, 2, 4, 32, 256)
    big = pltpu.VMEM(q.shape, BF16)
    full = jax.ShapeDtypeStruct(q.shape, BF16)
    return pl.pallas_call(
        lambda *refs: kernel(att_scale, grad_scale, *refs),
        out_shape=(full, full, jax.ShapeDtypeStruct((2, 4, 4, 32, width), BF16), jax.ShapeDtypeStruct(master.shape, F32)),
        in_specs=[ANY] * 5 + [VMEM] * 3,
        out_specs=(ANY, ANY, ANY, VMEM),
        scratch_shapes=[
            big, big, big, big, big, big, big, big, big, big,
            pltpu.VMEM((width, width), F32),
            pltpu.VMEM((2 * H, 3, HALF, HALF), BF16),
            pltpu.VMEM((H, HD, HD), BF16),
            pltpu.VMEM((H, HD, HD), F32),
            pltpu.VMEM((2, PLANE) + piece, BF16),
            pltpu.VMEM((2, PLANE) + piece, BF16),
            pltpu.VMEM((2, PLANE) + piece, F32),
            pltpu.VMEM((2,) + piece, BF16),
            pltpu.VMEM((2, GROUP) + piece, BF16),
            pltpu.VMEM((2, PLANE) + piece, BF16),
            pltpu.VMEM((2, PLANE) + piece, BF16),
            pltpu.VMEM((2, 4, 4, 2, 2) + tile, BF16),
            pltpu.VMEM((2, 4, 4, 2, 2) + tile, F32),
            pltpu.VMEM((2, 4, 4, 2, 2) + tile, BF16),
            pltpu.VMEM((2, 6, 2, 2, 2) + tile, BF16),
            pltpu.VMEM((2, 6, 2, 2, 2) + tile, BF16),
            pltpu.VMEM((2, 4, 2, 2) + tile, BF16),
            pltpu.VMEM((2, 4, 2, 2) + tile, BF16),
            pltpu.VMEM((4, 2, 2) + tile, BF16),
            pltpu.VMEM((2, 2, 2) + tile, BF16),
            pltpu.VMEM((2, 2, 2) + tile, F32),
            pltpu.VMEM((2, 2) + tile, F32),
            pltpu.VMEM((2, 2) + tile, F32),
            pltpu.VMEM(wide, BF16),
            pltpu.VMEM(wide, BF16),
            dma((5,)), dma((18,)),
            dma((2, PLANE)), dma((2, PLANE)), dma((2, GROUP)), dma((2, GROUP)), dma((2, PLANE)), dma((2, PLANE)),
            dma((2,)), dma((2,)), dma((2, 6)), dma((2, 6)), dma((2, 4)), dma((2, 4)),
            dma((4,)), dma((4,)), dma((2, 2, 4)), dma((2, 2, 4)),
            dma((2, 6)), dma((2, 6)), dma((2, 4)), dma((2, 4)), dma((2,)),
        ],
        compiler_params=pltpu.CompilerParams(collective_id=0, has_side_effects=True, vmem_limit_bytes=56 << 20),
        name="backward",
    )(inputs, q, k, v, g, master, m1, m2)


def local(inputs, queries, keys, values, out_grad, master, moment1, moment2):
    total_tokens = inputs.shape[0] * lax.axis_size("outer") * lax.axis_size("inner")
    att_scale = 1.0 / math.sqrt(HD * total_tokens)
    grad_scale = 1.0 / math.sqrt(total_tokens)
    query_grad, key_grad, weights, grad = kernel_call(
        att_scale, grad_scale, inputs, queries, keys, values, out_grad, master, moment1, moment2
    )
    new_master, first, second = adam(grad, master, moment1, moment2)
    return query_grad, key_grad, new_master, first, second, weights.reshape(inputs.shape[1], -1)


def solution(mesh):
    tokens, shard = P(("outer", "inner"), None), P("inner", None)
    return jax.shard_map(
        local,
        mesh=mesh,
        in_specs=(tokens,) * 5 + (shard,) * 3,
        out_specs=(tokens, tokens, shard, shard, shard, P()),
        check_vma=False,
    )
```

time: 1400 us -> 78.7 us (0.06)
  waiting for transfers between devices: 952 us -> 0 us
  other arithmetic: 321 us -> 1.69 us
  Pallas kernels: 0 us -> 69.2 us
  local copies, waits for them, and re-layouts: 60.2 us -> 6.91 us
  matrix products: 36.5 us -> 0 us
    all_gather x3 -> x0, waiting for transfers between devices: 738 us -> none  [the longest x2 738 us: entering(): everything = lax.all_gather(array, axis)]
    select_n x256 -> x0, other arithmetic: 314 us -> none  [turn(): return jnp.where(reached, new, before)]
    reduce_scatter x1 -> x0, waiting for transfers between devices: 166 us -> none  [local(): lax.psum_scatter(product * grad_scale, 'inner', scatter_dimension=0, tile...]
    pallas_call x0 -> x1, Pallas kernels: none -> 69.2 us  [kernel_call(): pl.pallas_call(lambda *refs: kernel(att_scale, grad_scale, *refs), out_sh...]
    psum x1 -> x0, waiting for transfers between devices: 48.4 us -> none  [local(): grad = lax.psum(shares, 'outer')]
    dot_general x17 -> x0, matrix products: 36.5 us -> none  [the longest x2 8.47 us: local(): jnp.einsum('thv,shv->hts', block_gradient, value_block_rows, preferred_el...]
    unnamed x60 -> x13, local copies, waits for them, and re-layouts: 33 us -> 6.91 us
    slice x9 -> x0, local copies, waits for them, and re-layouts: 17.3 us -> none  [the longest x3 7.58 us: local(): query_b = query_blocks[block_number]]
  transfers between devices with their start and end apart: 5 -> 0, of which waited for: 4 -> 0; matrix products, arithmetic and copies ran while one was open for 15% -> 0% of each run, Pallas kernels for 0% -> 0%
where the time goes in v2:
time: 78.7 us; the launch traced here: 78.5 us
  Pallas kernels  69.2 us (88%)
  local copies, waits for them, and re-layouts  6.91 us (9%)
  other arithmetic  1.69 us (2%)
    pallas_call x1, Pallas kernels, kernel_call(): pl.pallas_call(lambda *refs: kernel(att_scale, grad_scale, *refs), out_sh...  69.2 us
    unnamed x13, local copies, waits for them, and re-layouts  6.91 us
    sub x1, other arithmetic, adam(): new = master - 0.01 * (first / (jnp.sqrt(second) + 1e-08) + 0.1 * master)  1.69 us

profile of v2, /device:TPU:1, one launch (start us, length us, event | category | flops | bytes accessed | tf_op | source)
XLA Modules:
  0.0 78.5 jit_solution(12870653713853995215)
XLA Ops:
  0.6 0.0 copy-start.4
  0.6 0.0 copy-start.3
  0.7 0.0 copy-start.2
  0.7 69.2 %backward.1 = (bf16[1024,1024]{1,0:T(8,128)(2,1)}, bf16[1024,1024]{1,0:T(8,128)(2,1)}, bf16[2,4,4,32,1024]{4,3,2,1,0:T(8,128)(2,1)}, f32[32,1024]{1,0:T(8,128)}) custom-call(bf16[1024,1024]{1,0:T(8,128)(2,1)} %refs_0_.1, bf16[1024,1024]{1,0:T(8,128)(2,1)} %refs_1_.1, bf16[1024,1024]{1,0:T(8,128)(2,1)} %refs_2_.1, bf16[1024,1024]{1,0:T(8,128)(2,1)} %refs_3_.1, ...), custom_call_target="tpu_custom_call" | custom-call | tf_op jit(solution)/shard_map/backward/pallas_call | solution.py:453
  69.9 0.0 copy-done.4
  69.9 0.0 copy-done.3
  69.9 0.0 copy-done.2
  69.9 1.7 %multiply_subtract_fusion = (f32[32,1024]{1,0:T(8,128)}, f32[32,1024]{1,0:T(8,128)}, f32[32,1024]{1,0:T(8,128)}) fusion(f32[32,1024]{1,0:T(8,128)S(1)} %copy-done.2, f32[32,1024]{1,0:T(8,128)} %get-tuple-element.12, f32[32,1024]{1,0:T(8,128)S(1)} %copy-done.4, f32[32,1024]{1,0:T(8,128)S(1)} %copy-done.3), kind=kLoop, calls=%fused_computation.2 | loop fusion | flops 425984 | bytes 917504 | tf_op jit(solution)/shard_map/sub | solution.py:61
  71.6 0.0 copy-start.1
  71.6 3.2 %copy.17 = bf16[1024,1024]{1,0:T(8,128)(2,1)} copy(bf16[1024,1024]{1,0:T(8,128)(2,1)} %get-tuple-element.23) | data formatting | bytes 4194304
  74.8 0.0 copy-done.1
  74.8 0.0 copy-start
  74.8 1.3 %copy.18 = bf16[1024,1024]{1,0:T(8,128)(2,1)} copy(bf16[1024,1024]{1,0:T(8,128)(2,1)S(1)} %copy-done.1) | data formatting | bytes 4194304
  76.2 1.0 %copy-done = bf16[2,4,4,32,1024]{4,3,2,1,0:T(8,128)(2,1)S(1)} copy-done((bf16[2,4,4,32,1024]{4,3,2,1,0:T(8,128)(2,1)S(1)}, bf16[2,4,4,32,1024]{4,3,2,1,0:T(8,128)(2,1)}, u32[]{:S(2)}) %copy-start) | copy-done | bytes 2097176
  77.2 1.3 %copy.19 = bf16[1024,1024]{1,0:T(8,128)(2,1)} copy(bf16[1024,1024]{1,0:T(8,128)(2,1)S(1)} %bitcast.1) | data formatting | bytes 4194304
Async XLA Ops:
  0.6 69.3 %copy-start.4 = (f32[32,1024]{1,0:T(8,128)S(1)}, f32[32,1024]{1,0:T(8,128)}, u32[]{:S(2)}) copy-start(f32[32,1024]{1,0:T(8,128)} %refs_7_.1) | copy-start | bytes 393220
  0.6 69.3 %copy-start.3 = (f32[32,1024]{1,0:T(8,128)S(1)}, f32[32,1024]{1,0:T(8,128)}, u32[]{:S(2)}) copy-start(f32[32,1024]{1,0:T(8,128)} %refs_6_.1) | copy-start | bytes 393220
  0.7 69.3 %copy-start.2 = (f32[32,1024]{1,0:T(8,128)S(1)}, f32[32,1024]{1,0:T(8,128)}, u32[]{:S(2)}) copy-start(f32[32,1024]{1,0:T(8,128)} %refs_5_.1) | copy-start | bytes 393220
  71.6 3.2 %copy-start.1 = (bf16[1024,1024]{1,0:T(8,128)(2,1)S(1)}, bf16[1024,1024]{1,0:T(8,128)(2,1)}, u32[]{:S(2)}) copy-start(bf16[1024,1024]{1,0:T(8,128)(2,1)} %get-tuple-element.24) | copy-start | bytes 6291460
  74.8 2.3 %copy-start = (bf16[2,4,4,32,1024]{4,3,2,1,0:T(8,128)(2,1)S(1)}, bf16[2,4,4,32,1024]{4,3,2,1,0:T(8,128)(2,1)}, u32[]{:S(2)}) copy-start(bf16[2,4,4,32,1024]{4,3,2,1,0:T(8,128)(2,1)} %get-tuple-element.13) | copy-start | bytes 6291460

commit v3 on v2

--- a/solution.py
+++ b/solution.py
@@ -12,12 +12,13 @@
 BLK = 512
 HALF = BLK // 2
 PLANE = 16
-N1, N2, K1, M1, M2 = 6, 10, 4, 4, 10
+N1, N2, M1, M2, VM = 6, 10, 4, 10, 47
 GROUP = 8
 MESH = pl.DeviceIdType.MESH
 F32 = jnp.float32
 BF16 = jnp.bfloat16
 ANY = pl.BlockSpec(memory_space=pl.ANY)
+HBM = pl.BlockSpec(memory_space=pltpu.HBM)
 VMEM = pl.BlockSpec(memory_space=pltpu.VMEM)
 
 
@@ -69,9 +70,9 @@
 
 def kernel(
     att_scale, grad_scale,
-    x_hbm, q_hbm, k_hbm, v_hbm, g_hbm, master, m1, m2,
+    x_hbm, q_hbm, k_hbm, v_hbm, g_hbm, master_hbm, m1_hbm, m2_hbm,
     dq_hbm, dk_hbm, w_hbm, grad_ref,
-    x, q, k, v, g, xt, ki, xv, dq, dk, pre, scores, qg1, kv0,
+    master, m1, m2, x, q, k, v, g, xt, ki, xv, dq, dk, pre, scores, qg1, kv0,
     own, got, local, total, totals, back, final,
     give, mine, r0, r1, b, r2, c, r3, w, done, summed, other_sum, wide, far,
     in_sem, out_sem, a1, e1, a2, e2, a3, e3,
@@ -97,7 +98,7 @@
     barrier = pltpu.get_barrier_semaphore()
     greet(barrier, peers)
     loads = []
-    for n, (src, dst) in enumerate(((g_hbm, g), (q_hbm, q), (k_hbm, k), (v_hbm, v), (x_hbm, x))):
+    for n, (src, dst) in enumerate(((g_hbm, g), (q_hbm, q), (k_hbm, k), (v_hbm, v), (x_hbm, x), (master_hbm, master), (m1_hbm, m1), (m2_hbm, m2))):
         copy = pltpu.make_async_copy(src, dst, in_sem.at[n])
         copy.start()
         loads.append(copy)
@@ -215,48 +216,50 @@
             (nn(scores[step, 1], k0) + nn(scores[step, 2], k1) + nt(g[low, cols], state)) * att_scale
         ).astype(BF16)
 
-    def band_and_pair(step, half):
-        pair = half * 2 + step % 2
-        return pl.ds(pl.multiple_of((step // 2) * 256, 256), 256), pl.ds(pl.multiple_of(pair * 256, 256), 256), pair
-
-    def before_scan(half, whole):
-        def body(step):
-            band, cols, pair = band_and_pair(step, half)
-            upper = nn(xt[band, 0:BLK], v[0:BLK, cols])
-            lower = nn(xt[band, BLK : 2 * BLK], v[BLK : 2 * BLK, cols])
-            xv[band, cols] = (upper + lower).astype(BF16)
-            known = nn(upper.astype(BF16), diagonal(qg1[2 * pair], qg1[2 * pair + 1]))
-            if whole:
-                known = known + nn(xt[band, :], ki[:, cols])
-            pre[band, cols] = known
-
-        return body
-
-    def rest_of(half):
-        def body(step):
-            band, cols, pair = band_and_pair(step, half)
-            pre[band, cols] = pre[band, cols] + nn(xt[band, :], ki[:, cols])
-
-        return body
-
-    def after_scan(half, color, keep):
-        pair = half * 2 + color
+    def before_scan(step):
+        pair = (1 - core) * 2 + step % 2
+        band = pl.ds(pl.multiple_of((step // 2) * 256, 256), 256)
+        cols = pl.ds(pl.multiple_of(pair * 256, 256), 256)
+        upper = nn(xt[band, 0:BLK], v[0:BLK, cols])
+        lower = nn(xt[band, BLK : 2 * BLK], v[BLK : 2 * BLK, cols])
+        xv[band, cols] = (upper + lower).astype(BF16)
+        pre[band, cols] = nn(xt[band, :], ki[:, cols]) + nn(
+            upper.astype(BF16), diagonal(qg1[2 * pair], qg1[2 * pair + 1])
+        )
+
+    def lay(made, m, color, keep):
+        hi = m // 2
+        for part in range(8):
+            in_y, in_x = (m % 2) * 2 + part // 4, part % 4
+            for lo in range(2):
+                piece = made[part * 32 : part * 32 + 32, lo * 128 : lo * 128 + 128].astype(keep.dtype)
+                if color == 0:
+                    keep[color, in_x, in_y, hi, lo] = piece
+                else:
+                    keep[color, in_y, in_x, hi, lo] = piece
+
+    def after_scan(color):
+        pair = (1 - core) * 2 + color
         cols = pl.ds(pl.multiple_of(pair * 256, 256), 256)
         state = diagonal(state_of(QG, 2 * pair), state_of(QG, 2 * pair + 1))
 
-        @pl.loop(0, 4, unroll=2)
-        def _(m):
+        def body(m):
             band = pl.ds(pl.multiple_of(m * 256, 256), 256)
-            made = (pre[band, cols] + nn(xv[band, cols], state)) * (att_scale * grad_scale)
-            hi = m // 2
-            for part in range(8):
-                in_y, in_x = (m % 2) * 2 + part // 4, part % 4
-                for lo in range(2):
-                    piece = made[part * 32 : part * 32 + 32, lo * 128 : lo * 128 + 128].astype(keep.dtype)
-                    if color == 0:
-                        keep[color, in_x, in_y, hi, lo] = piece
-                    else:
-                        keep[color, in_y, in_x, hi, lo] = piece
+            lay((pre[band, cols] + nn(xv[band, cols], state)) * (att_scale * grad_scale), m, color, give)
+
+        return body
+
+    def product(color):
+        cols = pl.ds(pl.multiple_of((core * 2 + color) * 256, 256), 256)
+
+        def body(m):
+            band = pl.ds(pl.multiple_of(m * 256, 256), 256)
+            lay(nn(xt[band, :], dk[:, cols]) * grad_scale, m, color, mine)
+
+        return body
+
+    def key_pair(half, color):
+        return lambda step: key_end((step // 2) * H + half * 4 + color * 2 + step % 2)
 
     loads[0].wait()
     loads[1].wait()
@@ -266,14 +269,12 @@
     loads[2].wait()
     loads[3].wait()
     states(KV, k, v, kv0, 0)
-    spread(KV)
     loads[4].wait()
     pl.loop(0, N1, unroll=2)(key_side)
     gather(QG)
     share(QG)
+    spread(KV)
     pl.loop(N1, N2, unroll=2)(key_side)
-    gather(KV)
-    share(KV)
     answer(QG)
 
     @pl.loop(0, 4)
@@ -282,17 +283,15 @@
         xt[band, :] = x[:, band].T
 
     pl.loop(N2, 16, unroll=2)(key_side)
+    gather(KV)
+    share(KV)
+    pl.loop(0, 8, unroll=2)(before_scan)
+    answered(QG)
+
+    for color in range(2):
+        pl.loop(0, 4, unroll=2)(after_scan(color))
+        sent.append(send(give.at[color], r0.at[color], s0.at[color], q0.at[color], partner))
     answer(KV)
-    pl.loop(0, 8, unroll=2)(before_scan(1 - core, True))
-    pl.loop(0, 8, unroll=2)(before_scan(core, False))
-    answered(QG)
-
-    for color in range(2):
-        after_scan(1 - core, color, give)
-        sent.append(send(give.at[color], r0.at[color], s0.at[color], q0.at[color], partner))
-    pl.loop(0, 8, unroll=2)(rest_of(core))
-    for color in range(2):
-        after_scan(core, color, mine)
 
     lines = ((at_x, along_x), (at_y, along_y))
     def ahead(color, n, to, rows, peer, relay=None):
@@ -306,6 +305,8 @@
     first, second = slice(0, 2), slice(2, 4)
     for color in range(2):
         here, line = lines[color]
+        pl.loop(0, 4, unroll=2)(key_pair(core, color))
+        pl.loop(0, 4, unroll=2)(product(color))
         arrived(r0.at[color], q0.at[color])
         up, across, down = (here + 1) % 4, (here + 2) % 4, (here + 3) % 4
         ahead(color, 0, across, first, line[0])
@@ -313,12 +314,11 @@
         ahead(color, 2, up, second, line[0])
         ahead(color, 4, down, first, line[2])
         mine[color, here] = mine[color, here] + r0[color, here].astype(F32)
-    pl.loop(0, K1, unroll=2)(key_end)
     for color in range(2):
         here, line = lines[color]
         ahead(color, 3, (here + 1) % 4, first, line[0], 0)
         ahead(color, 5, (here + 3) % 4, second, line[2], 1)
-    pl.loop(K1, 16, unroll=2)(key_end)
+        pl.loop(0, 4, unroll=2)(key_pair(1 - core, color))
     outs = []
     copy = pltpu.make_async_copy(dk, dk_hbm, out_sem.at[16])
     copy.start()
@@ -350,6 +350,8 @@
         sent.append(send(w.at[to // 2], r3.at[o], s3.at[o], q3.at[o], peer))
     for o in range(1, 4):
         arrived(r3.at[o], q3.at[o])
+    for load in loads[5:]:
+        load.wait()
     summed[...] = done[z_hi] + r3[1].astype(F32) + r3[2].astype(F32) + r3[3].astype(F32)
     fresh = []
     for t in range(4):
@@ -453,9 +455,10 @@
     return pl.pallas_call(
         lambda *refs: kernel(att_scale, grad_scale, *refs),
         out_shape=(full, full, jax.ShapeDtypeStruct((2, 4, 4, 32, width), BF16), jax.ShapeDtypeStruct(master.shape, F32)),
-        in_specs=[ANY] * 5 + [VMEM] * 3,
+        in_specs=[HBM] * 8,
         out_specs=(ANY, ANY, ANY, VMEM),
         scratch_shapes=[
+            pltpu.VMEM(master.shape, F32), pltpu.VMEM(master.shape, F32), pltpu.VMEM(master.shape, F32),
             big, big, big, big, big, big, big, big, big, big,
             pltpu.VMEM((width, width), F32),
             pltpu.VMEM((2 * H, 3, HALF, HALF), BF16),
@@ -482,15 +485,15 @@
             pltpu.VMEM((2, 2) + tile, F32),
             pltpu.VMEM(wide, BF16),
             pltpu.VMEM(wide, BF16),
-            dma((5,)), dma((18,)),
+            dma((8,)), dma((18,)),
             dma((2, PLANE)), dma((2, PLANE)), dma((2, GROUP)), dma((2, GROUP)), dma((2, PLANE)), dma((2, PLANE)),
             dma((2,)), dma((2,)), dma((2, 6)), dma((2, 6)), dma((2, 4)), dma((2, 4)),
             dma((4,)), dma((4,)), dma((2, 2, 4)), dma((2, 2, 4)),
             dma((2, 6)), dma((2, 6)), dma((2, 4)), dma((2, 4)), dma((2,)),
         ],
-        compiler_params=pltpu.CompilerParams(collective_id=0, has_side_effects=True, vmem_limit_bytes=56 << 20),
+        compiler_params=pltpu.CompilerParams(collective_id=0, has_side_effects=True, vmem_limit_bytes=VM << 20),
         name="backward",
-    )(inputs, q, k, v, g, master, m1, m2)
+    )(*[pltpu.with_memory_space_constraint(a, pltpu.HBM) for a in (inputs, q, k, v, g, master, m1, m2)])
 
 
 def local(inputs, queries, keys, values, out_grad, master, moment1, moment2):

time: 78.7 us -> 70.5 us (0.90)
  Pallas kernels: 69.2 us -> 65 us
  local copies, waits for them, and re-layouts: 6.91 us -> 3.97 us
  other arithmetic: 1.69 us -> 0.79 us
    pallas_call x1, Pallas kernels: 69.2 us -> 65 us  [kernel_call(): pl.pallas_call(lambda *refs: kernel(att_scale, grad_scale, *refs), out_sh...]
    unnamed x13 -> x9, local copies, waits for them, and re-layouts: 6.91 us -> 3.97 us
    sub x1, other arithmetic: 1.69 us -> 0.79 us  [adam(): new = master - 0.01 * (first / (jnp.sqrt(second) + 1e-08) + 0.1 * master)]
where the time goes in v3:
time: 70.5 us; the launch traced here: 70.4 us
  Pallas kernels  65 us (92%)
  local copies, waits for them, and re-layouts  3.97 us (6%)
  other arithmetic  0.79 us (1%)
    pallas_call x1, Pallas kernels, kernel_call(): pl.pallas_call(lambda *refs: kernel(att_scale, grad_scale, *refs), out_sh...  65 us
    unnamed x9, local copies, waits for them, and re-layouts  3.97 us

profile of v3, /device:TPU:1, one launch (start us, length us, event | category | flops | bytes accessed | tf_op | source)
XLA Modules:
  0.0 70.4 jit_solution(4716709104301122402)
XLA Ops:
  0.6 0.0 copy-start.2
  0.6 0.0 copy-start.1
  0.7 0.0 copy-start
  0.7 65.0 %backward.1 = (bf16[1024,1024]{1,0:T(8,128)(2,1)S(1)}, bf16[1024,1024]{1,0:T(8,128)(2,1)S(1)}, bf16[2,4,4,32,1024]{4,3,2,1,0:T(8,128)(2,1)S(1)}, f32[32,1024]{1,0:T(8,128)S(1)}) custom-call(bf16[1024,1024]{1,0:T(8,128)(2,1)} %refs_0_.1, bf16[1024,1024]{1,0:T(8,128)(2,1)} %refs_1_.1, bf16[1024,1024]{1,0:T(8,128)(2,1)} %refs_2_.1, bf16[1024,1024]{1,0:T(8,128)(2,1)} %refs_3_.1, ...), custom_call_target="tpu_custom_call" | custom-call | tf_op jit(solution)/shard_map/backward/pallas_call | solution.py:455
  65.6 0.0 copy-done.2
  65.6 0.0 copy-done.1
  65.7 0.0 copy-done
  65.7 0.8 %multiply_subtract_fusion = (f32[32,1024]{1,0:T(8,128)}, f32[32,1024]{1,0:T(8,128)}, f32[32,1024]{1,0:T(8,128)}) fusion(f32[32,1024]{1,0:T(8,128)S(1)} %copy-done, f32[32,1024]{1,0:T(8,128)S(1)} %get-tuple-element.12, f32[32,1024]{1,0:T(8,128)S(1)} %copy-done.2, f32[32,1024]{1,0:T(8,128)S(1)} %copy-done.1), kind=kLoop, calls=%fused_computation.2 | loop fusion | flops 425984 | bytes 917504 | tf_op jit(solution)/shard_map/sub | solution.py:62
  66.5 1.3 %copy.17 = bf16[1024,1024]{1,0:T(8,128)(2,1)} copy(bf16[1024,1024]{1,0:T(8,128)(2,1)S(1)} %get-tuple-element.23) | data formatting | bytes 4194304
  67.8 1.3 %copy.18 = bf16[1024,1024]{1,0:T(8,128)(2,1)} copy(bf16[1024,1024]{1,0:T(8,128)(2,1)S(1)} %get-tuple-element.24) | data formatting | bytes 4194304
  69.1 1.3 %copy.19 = bf16[1024,1024]{1,0:T(8,128)(2,1)} copy(bf16[1024,1024]{1,0:T(8,128)(2,1)S(1)} %bitcast.1) | data formatting | bytes 4194304
Async XLA Ops:
  0.6 65.0 %copy-start.2 = (f32[32,1024]{1,0:T(8,128)S(1)}, f32[32,1024]{1,0:T(8,128)}, u32[]{:S(2)}) copy-start(f32[32,1024]{1,0:T(8,128)} %refs_7_.1) | copy-start | bytes 393220
  0.6 65.0 %copy-start.1 = (f32[32,1024]{1,0:T(8,128)S(1)}, f32[32,1024]{1,0:T(8,128)}, u32[]{:S(2)}) copy-start(f32[32,1024]{1,0:T(8,128)} %refs_6_.1) | copy-start | bytes 393220
  0.7 65.0 %copy-start = (f32[32,1024]{1,0:T(8,128)S(1)}, f32[32,1024]{1,0:T(8,128)}, u32[]{:S(2)}) copy-start(f32[32,1024]{1,0:T(8,128)} %refs_5_.1) | copy-start | bytes 393220

commit v4 on v3

--- a/solution.py
+++ b/solution.py
@@ -12,7 +12,7 @@
 BLK = 512
 HALF = BLK // 2
 PLANE = 16
-N1, N2, M1, M2, VM = 6, 10, 4, 10, 47
+N1, N2, M1, M2, M3, VM = 6, 10, 8, 10, 12, 47
 GROUP = 8
 MESH = pl.DeviceIdType.MESH
 F32 = jnp.float32
@@ -94,22 +94,29 @@
     beside_outer, beside_inner = (beside % 2) * 2 + core, (beside // 2) * PLANE
     near_x = [(beside_outer, beside_inner + at_y * 4 + (at_x + o) % 4) for o in range(4)]
     near_y = [(beside_outer, beside_inner + ((at_y + o) % 4) * 4 + at_x) for o in range(4)]
-    peers = plane + ranked + near_x[1:] + near_y[1:]
+    far_first = (10, 6, 9, 11, 5, 7, 13, 14, 15, 1, 2, 3, 8, 4, 12)
+    peers = [plane[o - 1] for o in far_first] + near_x[1:] + near_y[1:] + ranked
     barrier = pltpu.get_barrier_semaphore()
+    loads = []
+
+    def load(*pairs):
+        for src, dst in pairs:
+            copy = pltpu.make_async_copy(src, dst, in_sem.at[len(loads)])
+            copy.start()
+            loads.append(copy)
+
+    for side in range(2):
+        cols = slice(side * H // 2 * HD, (side + 1) * H // 2 * HD)
+        load((g_hbm.at[:, cols], g.at[:, cols]), (q_hbm.at[:, cols], q.at[:, cols]))
     greet(barrier, peers)
-    loads = []
-    for n, (src, dst) in enumerate(((g_hbm, g), (q_hbm, q), (k_hbm, k), (v_hbm, v), (x_hbm, x), (master_hbm, master), (m1_hbm, m1), (m2_hbm, m2))):
-        copy = pltpu.make_async_copy(src, dst, in_sem.at[n])
-        copy.start()
-        loads.append(copy)
     sent = []
     QG, KV = 0, 1
 
     def head_cols(h):
         return pl.ds(pl.multiple_of(h * HD, HD), HD)
 
-    def states(stream, left, right, keep, kept):
-        @pl.loop(0, H)
+    def states(stream, left, right, keep, kept, heads):
+        @pl.loop(*heads, unroll=2)
         def _(h):
             cols = head_cols(h)
             blocks = [tn(left[n * BLK : (n + 1) * BLK, cols], right[n * BLK : (n + 1) * BLK, cols]) for n in range(2)]
@@ -263,13 +270,18 @@
 
     loads[0].wait()
     loads[1].wait()
-    states(QG, g, q, qg1, 1)
+    states(QG, g, q, qg1, 1, (0, H // 2))
+    loads[2].wait()
+    loads[3].wait()
+    load((k_hbm, k), (v_hbm, v), (x_hbm, x))
+    states(QG, g, q, qg1, 1, (H // 2, H))
     pl.semaphore_wait(barrier, len(peers))
     spread(QG)
-    loads[2].wait()
-    loads[3].wait()
-    states(KV, k, v, kv0, 0)
     loads[4].wait()
+    loads[5].wait()
+    states(KV, k, v, kv0, 0, (0, H))
+    loads[6].wait()
+    load((master_hbm, master), (m1_hbm, m1), (m2_hbm, m2))
     pl.loop(0, N1, unroll=2)(key_side)
     gather(QG)
     share(QG)
@@ -350,8 +362,8 @@
         sent.append(send(w.at[to // 2], r3.at[o], s3.at[o], q3.at[o], peer))
     for o in range(1, 4):
         arrived(r3.at[o], q3.at[o])
-    for load in loads[5:]:
-        load.wait()
+    for copy in loads[7:]:
+        copy.wait()
     summed[...] = done[z_hi] + r3[1].astype(F32) + r3[2].astype(F32) + r3[3].astype(F32)
     fresh = []
     for t in range(4):
@@ -370,24 +382,31 @@
         line = lines[1 - color][1]
         near = near_y if color == 0 else near_x
         spot = wide.at[color, here, z_hi, there]
-        for o in (2, 1, 3, 0):
-            if o:
-                sent.append(send(spot, spot, s4.at[color, 0, o], q4.at[color, 0, o], line[o - 1]))
+        for o in (2, 1, 3):
             sent.append(send(spot, spot, s4.at[color, 1, o], q4.at[color, 1, o], near[o]))
+            sent.append(send(spot, spot, s4.at[color, 0, o], q4.at[color, 0, o], line[o - 1]))
+        sent.append(send(spot, spot, s4.at[color, 1, 0], q4.at[color, 1, 0], near[0]))
     sent.append(send(summed, other_sum, pair_sem.at[0], pair_sem.at[1], partner))
-    def onward(color, n, src, hi, peer):
-        spot = wide.at[color, src, hi]
-        sent.append(send(spot, spot, s5.at[color, n], q5.at[color, n], peer))
+    def quarter(color, src, near, part):
+        return wide.at[color, src, (z_hi + near) % 2, pl.ds(2 * part, 2)]
+
+    def onward(color, src, near, part, way, hop):
+        spot = quarter(color, src, near, part)
+        n = near * 2 + part
+        peer = lines[color][1][2 * way]
+        sent.append(send(spot, spot, s5.at[color, hop, way, n], q5.at[color, hop, way, n], peer))
+
+    def landed(color, src, near, part, way, hop):
+        arrived(quarter(color, src, near, part), q5.at[color, hop, way, near * 2 + part])
 
     for near in range(2):
-        hi = (z_hi + near) % 2
         for color in range(2):
             here, there = lines[color][0], lines[1 - color][0]
-            line = lines[color][1]
             for o in range(near == 0, 4):
-                arrived(wide.at[color, here, hi, (there + 4 - o) % 4], q4.at[color, near, o])
-            onward(color, 2 * near, here, hi, line[2 * near])
-            onward(color, 2 * near + 1, here, hi, line[2 - 2 * near])
+                arrived(wide.at[color, here, (z_hi + near) % 2, (there + 4 - o) % 4], q4.at[color, near, o])
+            for turn in range(2):
+                for way in range(2):
+                    onward(color, here, near, (way + turn) % 2, way, 0)
     for color in range(2):
         here = lines[color][0]
         sent.append(send(wide.at[color, here], far.at[color, here], s6.at[color, 0], q6.at[color, 0], partner))
@@ -400,16 +419,18 @@
         outs.append(copy)
 
     pl.loop(M1, M2, unroll=2)(query_end)
-    for color in range(2):
-        here, line = lines[color]
-        put(wide.at[color, here], core, color, here, color * 8)
-        arrived(wide.at[color, (here + 3) % 4, z_hi], q5.at[color, 0])
-        onward(color, 4, (here + 3) % 4, z_hi, line[0])
-    for color in range(2):
-        here, line = lines[color]
-        arrived(wide.at[color, (here + 1) % 4, 1 - z_hi], q5.at[color, 2])
-        onward(color, 5, (here + 1) % 4, 1 - z_hi, line[2])
-    pl.loop(M2, 16, unroll=2)(query_end)
+    for near in range(2):
+        for color in range(2):
+            here = lines[color][0]
+            for way in range(2):
+                src = (here + 3 - 2 * way) % 4
+                landed(color, src, near, way, way, 0)
+                onward(color, src, near, way, way, 1)
+        if near == 0:
+            pl.loop(M2, M3, unroll=2)(query_end)
+    for color in range(2):
+        put(wide.at[color, lines[color][0]], core, color, lines[color][0], color * 8)
+    pl.loop(M3, 16, unroll=2)(query_end)
     copy = pltpu.make_async_copy(dq, dq_hbm, out_sem.at[17])
     copy.start()
     outs.append(copy)
@@ -417,13 +438,13 @@
         for color in range(2):
             here = lines[color][0]
             src = (here + 4 - o) % 4
-            if o == 1:
-                arrived(wide.at[color, src, 1 - z_hi], q5.at[color, 3])
-            if o == 3:
-                arrived(wide.at[color, src, z_hi], q5.at[color, 1])
-            if o == 2:
-                arrived(wide.at[color, src, z_hi], q5.at[color, 4])
-                arrived(wide.at[color, src, 1 - z_hi], q5.at[color, 5])
+            for near in range(2):
+                if o == 2:
+                    for way in range(2):
+                        landed(color, src, near, way, way, 1)
+                else:
+                    way = o // 2
+                    landed(color, src, near, 1 - way, way, 0)
             sent.append(send(wide.at[color, src], far.at[color, src], s6.at[color, o], q6.at[color, o], partner))
             put(wide.at[color, src], core, color, src, color * 8 + o)
     for o in (0, 1, 3, 2):
@@ -485,15 +506,39 @@
             pltpu.VMEM((2, 2) + tile, F32),
             pltpu.VMEM(wide, BF16),
             pltpu.VMEM(wide, BF16),
-            dma((8,)), dma((18,)),
+            dma((10,)), dma((18,)),
             dma((2, PLANE)), dma((2, PLANE)), dma((2, GROUP)), dma((2, GROUP)), dma((2, PLANE)), dma((2, PLANE)),
             dma((2,)), dma((2,)), dma((2, 6)), dma((2, 6)), dma((2, 4)), dma((2, 4)),
             dma((4,)), dma((4,)), dma((2, 2, 4)), dma((2, 2, 4)),
-            dma((2, 6)), dma((2, 6)), dma((2, 4)), dma((2, 4)), dma((2,)),
+            dma((2, 2, 2, 4)), dma((2, 2, 2, 4)), dma((2, 4)), dma((2, 4)), dma((2,)),
         ],
         compiler_params=pltpu.CompilerParams(collective_id=0, has_side_effects=True, vmem_limit_bytes=VM << 20),
         name="backward",
     )(*[pltpu.with_memory_space_constraint(a, pltpu.HBM) for a in (inputs, q, k, v, g, master, m1, m2)])
+
+
+def finish(dq_in, dk_in, w_in, grad, master, m1, m2, dq, dk, w, new_master, new_m1, new_m2, sem):
+    copies = []
+    for n, (src, dst) in enumerate(((dq_in, dq), (dk_in, dk), (w_in, w))):
+        copy = pltpu.make_async_copy(src, dst, sem.at[n])
+        copy.start()
+        copies.append(copy)
+    new_master[...], new_m1[...], new_m2[...] = adam(grad[...], master[...], m1[...], m2[...])
+    for copy in copies:
+        copy.wait()
+
+
+def finish_call(dq, dk, w, grad, master, m1, m2):
+    shape = lambda a: jax.ShapeDtypeStruct(a.shape, a.dtype)
+    return pl.pallas_call(
+        finish,
+        out_shape=(shape(dq), shape(dk), shape(w), shape(master), shape(master), shape(master)),
+        in_specs=[ANY] * 3 + [VMEM] * 4,
+        out_specs=(ANY,) * 3 + (VMEM,) * 3,
+        scratch_shapes=[pltpu.SemaphoreType.DMA((3,))],
+        compiler_params=pltpu.CompilerParams(vmem_limit_bytes=4 << 20),
+        name="finish",
+    )(dq, dk, w, grad, master, m1, m2)
 
 
 def local(inputs, queries, keys, values, out_grad, master, moment1, moment2):
@@ -503,7 +548,9 @@
     query_grad, key_grad, weights, grad = kernel_call(
         att_scale, grad_scale, inputs, queries, keys, values, out_grad, master, moment1, moment2
     )
-    new_master, first, second = adam(grad, master, moment1, moment2)
+    query_grad, key_grad, weights, new_master, first, second = finish_call(
+        query_grad, key_grad, weights, grad, master, moment1, moment2
+    )
     return query_grad, key_grad, new_master, first, second, weights.reshape(inputs.shape[1], -1)
 
 

time: 70.5 us -> 68.8 us (0.976)
  local copies, waits for them, and re-layouts: 3.97 us -> 0.01 us
  Pallas kernels: 65 us -> 68 us
  other arithmetic: 0.79 us -> 0 us
    unnamed x9 -> x6, local copies, waits for them, and re-layouts: 3.97 us -> 0.01 us
    pallas_call x0 -> x1, Pallas kernels: none -> 3.47 us  [finish_call(): pl.pallas_call(finish, out_shape=(shape(dq), shape(dk), shape(w), shape(m...]
    sub x1 -> x0, other arithmetic: 0.79 us -> none  [adam(): new = master - 0.01 * (first / (jnp.sqrt(second) + 1e-08) + 0.1 * master)]
where the time goes in v4:
time: 68.8 us; the launch traced here: 68.7 us
  Pallas kernels  68 us (99%)
  between operations  0.69 us (1%)
    pallas_call x1, Pallas kernels, kernel_call(): pl.pallas_call(lambda *refs: kernel(att_scale, grad_scale, *refs), out_sh...  64.5 us
    pallas_call x1, Pallas kernels, finish_call(): pl.pallas_call(finish, out_shape=(shape(dq), shape(dk), shape(w), shape(m...  3.47 us

profile of v4, /device:TPU:1, one launch (start us, length us, event | category | flops | bytes accessed | tf_op | source)
XLA Modules:
  0.0 68.7 jit_solution(12458219172369236767)
XLA Ops:
  0.6 0.0 copy-start.2
  0.6 0.0 copy-start.1
  0.7 0.0 copy-start
  0.7 64.5 %backward.1 = (bf16[1024,1024]{1,0:T(8,128)(2,1)S(1)}, bf16[1024,1024]{1,0:T(8,128)(2,1)S(1)}, bf16[2,4,4,32,1024]{4,3,2,1,0:T(8,128)(2,1)S(1)}, f32[32,1024]{1,0:T(8,128)S(1)}) custom-call(bf16[1024,1024]{1,0:T(8,128)(2,1)} %refs_0_.1, bf16[1024,1024]{1,0:T(8,128)(2,1)} %refs_1_.1, bf16[1024,1024]{1,0:T(8,128)(2,1)} %refs_2_.1, bf16[1024,1024]{1,0:T(8,128)(2,1)} %refs_3_.1, ...), custom_call_target="tpu_custom_call" | custom-call | tf_op jit(solution)/shard_map/backward/pallas_call | solution.py:476
  65.2 0.0 copy-done.2
  65.2 0.0 copy-done.1
  65.2 0.0 copy-done
  65.2 3.5 %finish.1 = (bf16[1024,1024]{1,0:T(8,128)(2,1)}, bf16[1024,1024]{1,0:T(8,128)(2,1)}, bf16[2,4,4,32,1024]{4,3,2,1,0:T(8,128)(2,1)}, f32[32,1024]{1,0:T(8,128)}, f32[32,1024]{1,0:T(8,128)}, /*index=5*/f32[32,1024]{1,0:T(8,128)}) custom-call(bf16[1024,1024]{1,0:T(8,128)(2,1)S(1)} %get-tuple-element.16.dq_in, bf16[1024,1024]{1,0:T(8,128)(2,1)S(1)} %get-tuple-element.17.dk_in, ...), custom_call_target="tpu_custom_call" | custom-call | tf_op jit(solution)/shard_map/finish/pallas_call | solution.py:533
Async XLA Ops:
  0.6 64.6 %copy-start.2 = (f32[32,1024]{1,0:T(8,128)S(1)}, f32[32,1024]{1,0:T(8,128)}, u32[]{:S(2)}) copy-start(f32[32,1024]{1,0:T(8,128)} %m2.1) | copy-start | bytes 393220
  0.6 64.6 %copy-start.1 = (f32[32,1024]{1,0:T(8,128)S(1)}, f32[32,1024]{1,0:T(8,128)}, u32[]{:S(2)}) copy-start(f32[32,1024]{1,0:T(8,128)} %m1.1) | copy-start | bytes 393220
  0.7 64.6 %copy-start = (f32[32,1024]{1,0:T(8,128)S(1)}, f32[32,1024]{1,0:T(8,128)}, u32[]{:S(2)}) copy-start(f32[32,1024]{1,0:T(8,128)} %master.1) | copy-start | bytes 393220

commit v5 on v4

--- a/solution.py
+++ b/solution.py
@@ -12,7 +12,7 @@
 BLK = 512
 HALF = BLK // 2
 PLANE = 16
-N1, N2, M1, M2, M3, VM = 6, 10, 8, 10, 12, 47
+N1, M1, M2, M3, VM = 8, 4, 8, 12, 47
 GROUP = 8
 MESH = pl.DeviceIdType.MESH
 F32 = jnp.float32
@@ -116,7 +116,7 @@
         return pl.ds(pl.multiple_of(h * HD, HD), HD)
 
     def states(stream, left, right, keep, kept, heads):
-        @pl.loop(*heads, unroll=2)
+        @pl.loop(*heads, unroll=4)
         def _(h):
             cols = head_cols(h)
             blocks = [tn(left[n * BLK : (n + 1) * BLK, cols], right[n * BLK : (n + 1) * BLK, cols]) for n in range(2)]
@@ -172,12 +172,11 @@
         base = totals[stream, 0].astype(F32)
         for j in range(1, GROUP):
             base = base + totals[stream, j].astype(F32)
-        for j in range(PLANE):
-            back[stream, j] = (local[stream, j] + base).astype(BF16)
         for o in range(1, PLANE):
             to = (p + o) % PLANE
+            back[stream, to] = (local[stream, to] + base).astype(BF16)
             sent.append(send(back.at[stream, to], final.at[stream, p], a3.at[stream, o], e3.at[stream, p], plane[o - 1]))
-        final[stream, p] = back[stream, p]
+        final[stream, p] = (local[stream, p] + base).astype(BF16)
 
     def answered(stream):
         for o in range(1, PLANE):
@@ -282,11 +281,11 @@
     states(KV, k, v, kv0, 0, (0, H))
     loads[6].wait()
     load((master_hbm, master), (m1_hbm, m1), (m2_hbm, m2))
-    pl.loop(0, N1, unroll=2)(key_side)
+    pl.loop(0, N1, unroll=4)(key_side)
     gather(QG)
     share(QG)
     spread(KV)
-    pl.loop(N1, N2, unroll=2)(key_side)
+    pl.loop(N1, 16, unroll=4)(key_side)
     answer(QG)
 
     @pl.loop(0, 4)
@@ -294,17 +293,12 @@
         band = pl.ds(pl.multiple_of(m * 256, 256), 256)
         xt[band, :] = x[:, band].T
 
-    pl.loop(N2, 16, unroll=2)(key_side)
-    gather(KV)
-    share(KV)
-    pl.loop(0, 8, unroll=2)(before_scan)
+    pl.loop(0, 8, unroll=4)(before_scan)
     answered(QG)
 
     for color in range(2):
-        pl.loop(0, 4, unroll=2)(after_scan(color))
+        pl.loop(0, 4, unroll=4)(after_scan(color))
         sent.append(send(give.at[color], r0.at[color], s0.at[color], q0.at[color], partner))
-    answer(KV)
-
     lines = ((at_x, along_x), (at_y, along_y))
     def ahead(color, n, to, rows, peer, relay=None):
         part = mine[color, to, rows] + r0[color, to, rows].astype(F32)
@@ -317,8 +311,8 @@
     first, second = slice(0, 2), slice(2, 4)
     for color in range(2):
         here, line = lines[color]
-        pl.loop(0, 4, unroll=2)(key_pair(core, color))
-        pl.loop(0, 4, unroll=2)(product(color))
+        pl.loop(0, 4, unroll=4)(key_pair(core, color))
+        pl.loop(0, 4, unroll=4)(product(color))
         arrived(r0.at[color], q0.at[color])
         up, across, down = (here + 1) % 4, (here + 2) % 4, (here + 3) % 4
         ahead(color, 0, across, first, line[0])
@@ -326,17 +320,17 @@
         ahead(color, 2, up, second, line[0])
         ahead(color, 4, down, first, line[2])
         mine[color, here] = mine[color, here] + r0[color, here].astype(F32)
+    gather(KV)
+    share(KV)
     for color in range(2):
         here, line = lines[color]
         ahead(color, 3, (here + 1) % 4, first, line[0], 0)
         ahead(color, 5, (here + 3) % 4, second, line[2], 1)
-        pl.loop(0, 4, unroll=2)(key_pair(1 - core, color))
+        pl.loop(0, 4, unroll=4)(key_pair(1 - core, color))
     outs = []
     copy = pltpu.make_async_copy(dk, dk_hbm, out_sem.at[16])
     copy.start()
     outs.append(copy)
-    answered(KV)
-    pl.loop(0, M1, unroll=2)(query_end)
     for color in range(2):
         here = lines[color][0]
         there, line = lines[1 - color]
@@ -348,6 +342,7 @@
             to = (there + o) % 4
             c[color, o] = mine[color, here, to].astype(BF16)
             sent.append(send(c.at[color, o], r2.at[color, o], s2.at[color, o], q2.at[color, o], line[o - 1]))
+    answer(KV)
     for color in range(2):
         here, there = lines[color][0], lines[1 - color][0]
         for o in range(1, 4):
@@ -387,6 +382,8 @@
             sent.append(send(spot, spot, s4.at[color, 0, o], q4.at[color, 0, o], line[o - 1]))
         sent.append(send(spot, spot, s4.at[color, 1, 0], q4.at[color, 1, 0], near[0]))
     sent.append(send(summed, other_sum, pair_sem.at[0], pair_sem.at[1], partner))
+    answered(KV)
+    pl.loop(0, M1, unroll=4)(query_end)
     def quarter(color, src, near, part):
         return wide.at[color, src, (z_hi + near) % 2, pl.ds(2 * part, 2)]
 
@@ -418,7 +415,7 @@
         copy.start()
         outs.append(copy)
 
-    pl.loop(M1, M2, unroll=2)(query_end)
+    pl.loop(M1, M2, unroll=4)(query_end)
     for near in range(2):
         for color in range(2):
             here = lines[color][0]
@@ -427,10 +424,10 @@
                 landed(color, src, near, way, way, 0)
                 onward(color, src, near, way, way, 1)
         if near == 0:
-            pl.loop(M2, M3, unroll=2)(query_end)
+            pl.loop(M2, M3, unroll=4)(query_end)
     for color in range(2):
         put(wide.at[color, lines[color][0]], core, color, lines[color][0], color * 8)
-    pl.loop(M3, 16, unroll=2)(query_end)
+    pl.loop(M3, 16, unroll=4)(query_end)
     copy = pltpu.make_async_copy(dq, dq_hbm, out_sem.at[17])
     copy.start()
     outs.append(copy)
@@ -520,9 +517,12 @@
 def finish(dq_in, dk_in, w_in, grad, master, m1, m2, dq, dk, w, new_master, new_m1, new_m2, sem):
     copies = []
     for n, (src, dst) in enumerate(((dq_in, dq), (dk_in, dk), (w_in, w))):
-        copy = pltpu.make_async_copy(src, dst, sem.at[n])
-        copy.start()
-        copies.append(copy)
+        parts = src.shape[0] // 2
+        for side in range(2):
+            rows = slice(side * parts, (side + 1) * parts)
+            copy = pltpu.make_async_copy(src.at[rows], dst.at[rows], sem.at[2 * n + side])
+            copy.start()
+            copies.append(copy)
     new_master[...], new_m1[...], new_m2[...] = adam(grad[...], master[...], m1[...], m2[...])
     for copy in copies:
         copy.wait()
@@ -535,7 +535,7 @@
         out_shape=(shape(dq), shape(dk), shape(w), shape(master), shape(master), shape(master)),
         in_specs=[ANY] * 3 + [VMEM] * 4,
         out_specs=(ANY,) * 3 + (VMEM,) * 3,
-        scratch_shapes=[pltpu.SemaphoreType.DMA((3,))],
+        scratch_shapes=[pltpu.SemaphoreType.DMA((6,))],
         compiler_params=pltpu.CompilerParams(vmem_limit_bytes=4 << 20),
         name="finish",
     )(dq, dk, w, grad, master, m1, m2)

time: 68.8 us -> 66.5 us (0.967)
  Pallas kernels: 68 us -> 65.6 us
    pallas_call x1, Pallas kernels: 64.5 us -> 62.1 us  [kernel_call(): pl.pallas_call(lambda *refs: kernel(att_scale, grad_scale, *refs), out_sh...]
where the time goes in v5:
time: 66.5 us; the launch traced here: 66.4 us
  Pallas kernels  65.6 us (99%)
  between operations  0.85 us (1%)
    pallas_call x1, Pallas kernels, kernel_call(): pl.pallas_call(lambda *refs: kernel(att_scale, grad_scale, *refs), out_sh...  62.1 us
    pallas_call x1, Pallas kernels, finish_call(): pl.pallas_call(finish, out_shape=(shape(dq), shape(dk), shape(w), shape(m...  3.46 us

profile of v5, /device:TPU:1, one launch (start us, length us, event | category | flops | bytes accessed | tf_op | source)
XLA Modules:
  0.0 66.4 jit_solution(789362723552579766)
XLA Ops:
  0.6 0.0 copy-start.2
  0.6 0.0 copy-start.1
  0.7 0.0 copy-start
  0.7 62.1 %backward.1 = (bf16[1024,1024]{1,0:T(8,128)(2,1)S(1)}, bf16[1024,1024]{1,0:T(8,128)(2,1)S(1)}, bf16[2,4,4,32,1024]{4,3,2,1,0:T(8,128)(2,1)S(1)}, f32[32,1024]{1,0:T(8,128)S(1)}) custom-call(bf16[1024,1024]{1,0:T(8,128)(2,1)} %refs_0_.1, bf16[1024,1024]{1,0:T(8,128)(2,1)} %refs_1_.1, bf16[1024,1024]{1,0:T(8,128)(2,1)} %refs_2_.1, bf16[1024,1024]{1,0:T(8,128)(2,1)} %refs_3_.1, ...), custom_call_target="tpu_custom_call" | custom-call | tf_op jit(solution)/shard_map/backward/pallas_call | solution.py:473
  62.8 0.0 copy-done.2
  62.8 0.0 copy-done.1
  62.8 0.0 copy-done
  62.8 3.5 %finish.1 = (bf16[1024,1024]{1,0:T(8,128)(2,1)}, bf16[1024,1024]{1,0:T(8,128)(2,1)}, bf16[2,4,4,32,1024]{4,3,2,1,0:T(8,128)(2,1)}, f32[32,1024]{1,0:T(8,128)}, f32[32,1024]{1,0:T(8,128)}, /*index=5*/f32[32,1024]{1,0:T(8,128)}) custom-call(bf16[1024,1024]{1,0:T(8,128)(2,1)S(1)} %get-tuple-element.16.dq_in, bf16[1024,1024]{1,0:T(8,128)(2,1)S(1)} %get-tuple-element.17.dk_in, ...), custom_call_target="tpu_custom_call" | custom-call | tf_op jit(solution)/shard_map/finish/pallas_call | solution.py:533
Async XLA Ops:
  0.6 62.1 %copy-start.2 = (f32[32,1024]{1,0:T(8,128)S(1)}, f32[32,1024]{1,0:T(8,128)}, u32[]{:S(2)}) copy-start(f32[32,1024]{1,0:T(8,128)} %m2.1) | copy-start | bytes 393220
  0.6 62.1 %copy-start.1 = (f32[32,1024]{1,0:T(8,128)S(1)}, f32[32,1024]{1,0:T(8,128)}, u32[]{:S(2)}) copy-start(f32[32,1024]{1,0:T(8,128)} %m1.1) | copy-start | bytes 393220
  0.7 62.1 %copy-start = (f32[32,1024]{1,0:T(8,128)S(1)}, f32[32,1024]{1,0:T(8,128)}, u32[]{:S(2)}) copy-start(f32[32,1024]{1,0:T(8,128)} %master.1) | copy-start | bytes 393220
